TPU v7x, 32 devices: a whole 2x2x4 slice. The times are simulated.
32 devices in a mesh: groups: 2 (over x), ctx: 16 (over z, y, core).
Axes of the slice: x: 2, y: 2, z: 4, core: 2. Of those that a mesh axis runs over, the one named last changes fastest.
Arguments:
- queries: bfloat16 [4096, 2048], P(('groups', 'ctx')), parts along dimension 0, may hold values from -6 to 6
- keys: bfloat16 [8192, 256], P(('groups', 'ctx')), parts along dimension 0, may hold values from -6 to 6
- values: bfloat16 [8192, 256], P(('groups', 'ctx')), parts along dimension 0, may hold values from -6 to 6
- kv_lengths: int32 [32], P(('groups', 'ctx')), parts along dimension 0, may hold values from 1 to 256, 2048 in all
- stream: bfloat16 [4096, 2048], P(('groups', 'ctx')), parts along dimension 0, may hold values from -6 to 6
- out_weight: bfloat16 [2048, 2048], P('ctx'), may hold values from -0.125 to 0.125
- routes: int32 [4096, 8], P(('groups', 'ctx')), parts along dimension 0, may hold values from 0 to 15, all different within a row; in each aligned block of 128 rows (0 to 127, 128 to 255, ...) at most 72 rows name the same one
- gate_weights: float32 [4096, 8], P(('groups', 'ctx')), parts along dimension 0, may hold values from 0.2 to 1
- expert_gate: bfloat16 [16, 2048, 768], P('ctx'), may hold values from -0.125 to 0.125
- expert_up: bfloat16 [16, 2048, 768], P('ctx'), may hold values from -0.125 to 0.125
- expert_down: bfloat16 [16, 768, 2048], P('ctx'), may hold values from -0.21875 to 0.21875
Outputs:
- attended: bfloat16 [4096, 2048], P(('groups', 'ctx')), parts along dimension 0
- layer_out: bfloat16 [4096, 2048], P(('groups', 'ctx')), parts along dimension 0
There are 2 independent parts, one for each index of `groups`. A program takes and returns all parts, laid end to end along the dimension named above; an argument that names none is the same for every part. Nothing has to cross between parts.
Inputs may be any that keep to these rules, and one draw needn't show every extreme that they name: `routes`: in the rows of one device (aligned blocks of 128 rows) no expert is named by more than 72 entries.
All inputs are finite; a program needn't handle non-finite values. No bound on the sum of `kv_lengths` on one device may be relied on, other than what follows from the above.
Results may differ from a plain program's by a relative error of at most 0.015.
Values may be sent and summed in bfloat16 or wider, within the bound.
No kernel may reach another device: no remote copies, remote signals or barrier semaphores. Data moves between devices by JAX's collectives and lax.ppermute only.
A program may use at most 128 MiB of HBM per device.

v0:
```python
import functools
import math

import jax
import jax.numpy as jnp
from jax import lax
from jax.experimental import pallas as pl
from jax.experimental.pallas import tpu as pltpu
from jax.sharding import PartitionSpec as P


HD = 128
STOPS = 8
CORES = 2
DEAD = 1e30


def from_behind(block, axis, distance):
    devices = range(lax.axis_size(axis))
    route = [(i - distance, i) for i in devices if i - distance in devices]
    return lax.ppermute(block, axis, route)


def attend_kernel(heads, parts, length_ref, core_ref, q_ref, *refs):
    k_refs, v_refs, rest = refs[:parts], refs[parts : 2 * parts], refs[2 * parts :]
    o_ref, split_refs, bias_ref = rest[0], rest[1:-1], rest[-1]
    stops = length_ref.shape[0]
    kv_rows = bias_ref.shape[1] // stops
    rows = q_ref.shape[0]

    @pl.when(pl.program_id(0) == 0)
    def _():
        if split_refs:
            first_lane = lax.broadcasted_iota(jnp.int32, (16, HD), 1) == 0
            marks = lax.dot_general(
                first_lane.astype(jnp.float32).astype(jnp.bfloat16),
                jnp.concatenate([v_ref[...] for v_ref in v_refs], axis=0),
                (((1,), (1,)), ((), ())),
                preferred_element_type=jnp.float32,
            )[:1]
        row = lax.broadcasted_iota(jnp.int32, (1, kv_rows), 1)
        for stop in range(stops):
            part = slice(stop * kv_rows, (stop + 1) * kv_rows)
            if split_refs:
                dead = (marks[:, part] > DEAD / 2) | (row < kv_rows * (1 - length_ref[stop]))
            else:
                dead = row >= length_ref[stop]
            bias_ref[:, part] = jnp.where(dead, -1e30, 0.0)

    stacked = jnp.concatenate([q_ref[:, h * HD : (h + 1) * HD] for h in range(heads)], axis=0)
    scores = lax.dot_general(
        stacked,
        jnp.concatenate([k_ref[...] for k_ref in k_refs], axis=0),
        (((1,), (1,)), ((), ())),
        preferred_element_type=jnp.float32,
    )
    scores = scores * (HD ** (-0.5) * math.log2(math.e)) + bias_ref[...]
    highest = jnp.max(scores, axis=-1, keepdims=True)
    weights = jnp.exp2(scores - highest)
    total = jnp.sum(weights, axis=-1, keepdims=True)
    out = jnp.dot(
        weights.astype(jnp.bfloat16),
        jnp.concatenate([v_ref[...] for v_ref in v_refs], axis=0),
        preferred_element_type=jnp.float32,
    )
    out = (out / total).astype(o_ref.dtype)
    for h in range(heads):
        o_ref[:, h * HD : (h + 1) * HD] = out[h * rows : (h + 1) * rows]
    if split_refs:
        mine_ref, theirs_ref = split_refs
        first = core_ref[0] == 0
        mine_ref[...] = jnp.where(first, out[:rows], out[rows:])
        theirs_ref[...] = jnp.where(first, out[rows:], out[:rows])


def attend(queries, windows, lengths, core=None):
    rows, width = queries.shape
    kv_rows = sum(window.shape[0] for window in windows)
    kv_width = windows[0].shape[1]
    kv_heads = kv_width // (2 * HD)
    heads = width // HD
    pair = 2 if heads // kv_heads % 2 == 0 else 1
    group = heads // kv_heads // pair
    split = core is not None
    number = core if split else jnp.zeros((), jnp.int32)
    outs = [jax.ShapeDtypeStruct((rows, width), jnp.bfloat16)]
    outs += [jax.ShapeDtypeStruct((rows, width // 2), jnp.bfloat16)] * (2 * split)
    out_specs = [pl.BlockSpec((rows, pair * HD), lambda h, n, c: (0, h))]
    out_specs += [pl.BlockSpec((rows, HD), lambda h, n, c: (0, h))] * (2 * split)
    specs = [pl.BlockSpec((rows, pair * HD), lambda h, n, c: (0, h))]
    for first in (0, kv_heads):
        for window in windows:
            specs.append(
                pl.BlockSpec(
                    (window.shape[0], HD), lambda h, n, c, first=first: (0, first + h // group)
                )
            )
    return pl.pallas_call(
        functools.partial(attend_kernel, pair, len(windows)),
        grid_spec=pltpu.PrefetchScalarGridSpec(
            num_scalar_prefetch=2,
            grid=(heads // pair,),
            in_specs=specs,
            out_specs=out_specs,
            scratch_shapes=[pltpu.VMEM((1, kv_rows), jnp.float32)],
        ),
        out_shape=outs,
        compiler_params=pltpu.CompilerParams(vmem_limit_bytes=20 * 1024 * 1024),
        cost_estimate=pl.CostEstimate(
            flops=4 * rows * width * kv_rows,
            transcendentals=rows * heads * kv_rows,
            bytes_accessed=2 * (2 * rows * width + kv_rows * kv_width),
        ),
        name="attend",
    )(lengths, number.reshape(1), queries, *windows, *windows)


def key_window(keys, values):
    window = jnp.concatenate([keys, values], axis=1)
    held = 1
    while held < STOPS:
        window = jnp.concatenate([window, from_behind(window, "ctx", held)], axis=0)
        held *= 2
    return window


def expert_kernel(count, *refs):
    x_refs = refs[:count]
    factor_ref = refs[count]
    trios = (refs[count + 1 : count + 4], refs[count + 4 : count + 7])
    o_refs = refs[count + 7 :]
    x = jnp.concatenate([x_ref[...] for x_ref in x_refs], axis=0)
    total = None
    for column, (gate_ref, up_ref, down_ref) in enumerate(trios):
        gate = jnp.dot(x, gate_ref[0], preferred_element_type=jnp.float32)
        up = jnp.dot(x, up_ref[0], preferred_element_type=jnp.float32)
        hidden = gate / (1.0 + jnp.exp(-gate)) * up * factor_ref[:, column : column + 1]
        part = jnp.dot(hidden.astype(jnp.bfloat16), down_ref[0], preferred_element_type=jnp.float32)
        total = part if total is None else total + part
    low = 0
    for o_ref in o_refs:
        high = low + o_ref.shape[0]
        o_ref[...] = total[low:high].astype(o_ref.dtype)
        low = high


def run_experts(blocks, factors, own, other):
    width = blocks[0].shape[1]
    hidden = own[0].shape[2]
    rows = sum(block.shape[0] for block in blocks)
    count = len(blocks)
    held = pl.BlockSpec(memory_space=pltpu.VMEM)
    return pl.pallas_call(
        functools.partial(expert_kernel, count),
        in_specs=[held] * (count + 7),
        out_specs=[held] * count,
        out_shape=[jax.ShapeDtypeStruct(block.shape, jnp.bfloat16) for block in blocks],
        compiler_params=pltpu.CompilerParams(vmem_limit_bytes=20 * 1024 * 1024),
        cost_estimate=pl.CostEstimate(
            flops=12 * rows * width * hidden,
            transcendentals=2 * rows * hidden,
            bytes_accessed=12 * width * hidden + 4 * rows * width,
        ),
        name="experts",
    )(*blocks, factors, *own, *other)


def project(attended, weight, stream):
    projected = jnp.dot(attended, weight, preferred_element_type=jnp.float32)
    residual = (stream.astype(jnp.float32) + projected).astype(jnp.bfloat16)
    widened = residual.astype(jnp.float32)
    normed = (
        widened * lax.rsqrt(jnp.mean(widened * widened, axis=-1, keepdims=True) + 1e-06)
    ).astype(jnp.bfloat16)
    return widened, normed


def project_kernel(order_ref, mine_ref, got_ref, *refs):
    *pieces, keep_ref, give_ref = refs
    rows = mine_ref.shape[0]
    total = None
    for index in range(0, len(pieces), 2):
        columns = []
        for place in (index, index + 1):
            low = pl.multiple_of(order_ref[place] * HD, HD)
            columns.append(
                jnp.concatenate([mine_ref[:, pl.ds(low, HD)], got_ref[:, pl.ds(low, HD)]], axis=0)
            )
        part = jnp.dot(
            jnp.concatenate(columns, axis=1),
            jnp.concatenate([pieces[index][...], pieces[index + 1][...]], axis=0),
            preferred_element_type=jnp.float32,
        )
        total = part if total is None else total + part
    keep_ref[...] = total[:rows]
    give_ref[...] = total[rows:]


def project_pieces(mine, got, pieces, order):
    rows = mine.shape[0]
    width = pieces[0].shape[1]
    part = 512 if width % 512 == 0 else width
    whole = pl.BlockSpec(mine.shape, lambda i, n: (0, 0))
    wide = pl.BlockSpec((rows, part), lambda i, n: (0, i))
    like = jax.ShapeDtypeStruct((rows, width), jnp.float32)
    return pl.pallas_call(
        project_kernel,
        grid_spec=pltpu.PrefetchScalarGridSpec(
            num_scalar_prefetch=1,
            grid=(width // part,),
            in_specs=[whole, whole]
            + [pl.BlockSpec((piece.shape[0], part), lambda i, n: (0, i)) for piece in pieces],
            out_specs=[wide, wide],
        ),
        out_shape=[like, like],
        compiler_params=pltpu.CompilerParams(vmem_limit_bytes=20 * 1024 * 1024),
        cost_estimate=pl.CostEstimate(
            flops=4 * rows * width * mine.shape[1],
            transcendentals=0,
            bytes_accessed=2 * mine.shape[1] * width + 8 * rows * width,
        ),
        name="project",
    )(order, mine, got, *pieces)


def norm_kernel(stream_ref, keep_ref, got_ref, residual_ref, normed_ref):
    total = stream_ref[...].astype(jnp.float32) + keep_ref[...] + got_ref[...]
    residual = total.astype(jnp.bfloat16)
    residual_ref[...] = residual
    widened = residual.astype(jnp.float32)
    square = jnp.mean(widened * widened, axis=-1, keepdims=True)
    normed_ref[...] = (widened * lax.rsqrt(square + 1e-06)).astype(jnp.bfloat16)


def add_norm(stream, keep, got):
    rows, width = stream.shape
    like = jax.ShapeDtypeStruct(stream.shape, jnp.bfloat16)
    part = rows // 4 if rows % 64 == 0 else rows
    held = pl.BlockSpec((part, width), lambda i: (i, 0))
    return pl.pallas_call(
        norm_kernel,
        grid=(rows // part,),
        in_specs=[held] * 3,
        out_specs=[held, held],
        out_shape=[like, like],
        compiler_params=pltpu.CompilerParams(vmem_limit_bytes=20 * 1024 * 1024),
        name="add_norm",
    )(stream, keep, got)


def chip_ring(devices):
    chips = devices // CORES
    return list(range(0, chips, 2)) + list(range(1, chips, 2))[::-1]


def ring_layer(
    queries, keys, values, kv_lengths, stream, out_weight, routes, gate_weights, own
):
    rows = queries.shape[0]
    devices = lax.axis_size("ctx")
    here = lax.axis_index("ctx")
    ring = chip_ring(devices)
    span = len(ring)
    half = span // 2
    core, side = here % 2, here // 2 % 2
    flip = [[(i, i ^ bit) for i in range(devices)] for bit in (1, 2)]

    def moved(block, distance):
        route = [
            (ring[i] * CORES + c, ring[(i + distance) % span] * CORES + c)
            for i in range(span)
            for c in range(CORES)
        ]
        return lax.ppermute(block, "ctx", route)

    def swapped(block):
        return lax.ppermute(block, "ctx", flip[0])

    def far_memory(array):
        return pltpu.with_memory_space_constraint(array, pltpu.HBM)

    def near_memory(arrays):
        return [pltpu.with_memory_space_constraint(array, pltpu.VMEM) for array in arrays]

    chip = here // CORES
    my_place = jnp.where(chip % 2 == 0, chip // 2, span - 1 - chip // 2)
    offsets = [0] + [s * k for k in range(1, half) for s in (-1, 1)] + [half]
    places = (my_place + jnp.array(offsets, jnp.int32)) % span
    chips = jnp.where(places < half, 2 * places, 2 * (span - 1 - places) + 1)
    order = chips * CORES + core
    near = jnp.array([0, 4, 2, 6, 1, 5, 3, 7], jnp.int32)
    far = jnp.array([0, 4, 2, 6, 7, 3, 1, 5], jnp.int32)
    reached = (here - jnp.where(core == 1, near, far) >= 0).astype(jnp.int32)

    kv_rows = keys.shape[0]
    live = jnp.arange(kv_rows, dtype=jnp.int32)[:, None] < kv_lengths[0]
    expert = jnp.arange(devices, dtype=jnp.int32)
    named = routes.T[None] == expert[:, None, None]
    factor = jnp.sum(jnp.where(named, gate_weights.T[None], 0.0), axis=1)
    factor_swap = factor.reshape(devices // 2, 2, rows)[:, ::-1].reshape(devices, rows)
    notes = jnp.stack([factor, factor_swap], axis=1)

    ahead, back = moved(out_weight, 1), moved(out_weight, -1)
    mine = jnp.concatenate([keys, jnp.where(live, values, DEAD).astype(values.dtype)], axis=1)
    second = from_behind(mine, "ctx", 4)
    pieces = [out_weight]
    fourth = crossed = crossed_far = None
    for step in range(2, half + 1):
        if step == 2:
            second, ahead, back, notes, *late = lax.optimization_barrier(
                (second, ahead, back, notes, *own)
            )
            notes = lax.all_to_all(notes, "ctx", split_axis=0, concat_axis=0, tiled=True)
            fourth = from_behind(second, "ctx", 4)
            crossed = lax.ppermute(jnp.where(side == 0, mine, second), "ctx", flip[1])
            other = [swapped(weight) for weight in late]
        elif step == 3:
            fourth, crossed, ahead, back, notes = lax.optimization_barrier(
                (fourth, crossed, ahead, back, notes)
            )
            crossed_far = lax.ppermute(jnp.where(side == 0, second, fourth), "ctx", flip[1])
        else:
            ahead, back = lax.optimization_barrier((ahead, back))
        pieces += [far_memory(ahead), far_memory(back)]
        if step < half:
            ahead, back = moved(ahead, 1), moved(back, -1)
    if crossed_far is None:
        crossed_far = lax.ppermute(jnp.where(side == 0, second, fourth), "ctx", flip[1])
    windows = [mine, second, crossed, crossed_far]
    shared = [jnp.where(core == 0, mine, fourth), second, crossed, crossed_far]
    windows += [swapped(window) for window in shared]
    ahead, notes, *windows = lax.optimization_barrier((ahead, notes, *windows))
    last = moved(ahead, 1)
    pieces.append(far_memory(last))
    attended, kept, given = attend(queries, windows, reached, core)
    got = swapped(given)
    chosen = (order[:, None] == expert[None])[:, :, None, None]
    picked = jnp.sum(jnp.where(chosen, notes[None], 0.0), axis=1)
    picked = picked.transpose(0, 2, 1).reshape(-1, 2)

    own, other = near_memory(own), near_memory(other)
    keep, give = project_pieces(kept, got, pieces, chips)
    residual, normed = add_norm(stream, keep, swapped(give))

    def factors(first, number):
        return picked[first * rows : (first + number) * rows]

    cut = rows // 2
    (home,) = run_experts([normed], factors(0, 1), own, other)
    ahead, back = normed, normed
    done = [home]
    sums = []
    for step in range(1, half):
        ahead, back = moved(ahead, 1), moved(back, -1)
        ahead, back, *done = lax.optimization_barrier((ahead, back, *done))
        sums.append(done)
        done = run_experts([ahead, back], factors(2 * step - 1, 2), own, other)
    far_low, far_high = moved(ahead[:cut], 1), moved(back[cut:], -1)
    far_low, far_high, *done = lax.optimization_barrier((far_low, far_high, *done))
    sums.append(done)
    far_low, far_high = run_experts(
        [far_low, far_high], factors(2 * half - 1, 1), own, other
    )

    def summed(a, b):
        return (a.astype(jnp.float32) + b.astype(jnp.float32)).astype(jnp.bfloat16)

    got_low, got_high = moved(far_low, -1), moved(far_high, 1)
    for step in range(half - 1, 0, -1):
        mine_low, mine_high = sums[step]
        if step == half - 1:
            send_low = jnp.concatenate([summed(got_low, mine_low[:cut]), mine_low[cut:]])
            send_high = jnp.concatenate([mine_high[:cut], summed(got_high, mine_high[cut:])])
        else:
            send_low = summed(got_low, mine_low)
            send_high = summed(got_high, mine_high)
        got_low, got_high = moved(send_low, -1), moved(send_high, 1)
    (home,) = sums[0]
    mixture = (
        home.astype(jnp.float32) + got_low.astype(jnp.float32) + got_high.astype(jnp.float32)
    )
    return attended, (residual.astype(jnp.float32) + mixture).astype(jnp.bfloat16)


def slot_layer(
    queries, keys, values, kv_lengths, stream, out_weight, routes, gate_weights, own
):
    expert_gate, expert_up, expert_down = own
    row_count = queries.shape[0]
    cycle_size = lax.axis_size("ctx")
    weight_all = lax.all_gather(out_weight, "ctx", axis=0, tiled=True)
    lengths = kv_lengths
    held = 1
    while held < STOPS:
        lengths = jnp.concatenate([lengths, from_behind(lengths, "ctx", held)])
        held *= 2
    (attended,) = attend(queries, [key_window(keys, values)], lengths)
    widened, normed = project(attended, weight_all, stream)
    width = normed.shape[1]
    route_count = routes.shape[1]
    local_count = expert_gate.shape[0]
    expert_total = local_count * cycle_size
    capacity = slot_capacity(row_count, route_count, expert_total)
    flat_routes = routes.reshape(-1)
    one_hot = (flat_routes[:, None] == jnp.arange(expert_total, dtype=jnp.int32)[None, :]).astype(
        jnp.int32
    )
    earlier = jnp.cumsum(one_hot, axis=0) - one_hot
    slot_index = jnp.sum(earlier * one_hot, axis=1)
    slot_target = flat_routes * capacity + slot_index
    source_row = jnp.arange(row_count * route_count, dtype=jnp.int32) // route_count
    buffer_rows = jnp.zeros((expert_total * capacity,), jnp.int32).at[slot_target].set(source_row)
    buffer_live = jnp.zeros((expert_total * capacity,), jnp.bool_).at[slot_target].set(True)
    send_buffer = jnp.where(
        buffer_live[:, None], normed[buffer_rows], jnp.zeros((), jnp.bfloat16)
    ).reshape(expert_total, capacity, width)
    arrived = lax.all_to_all(send_buffer, "ctx", split_axis=0, concat_axis=0, tiled=True)
    by_source = arrived.reshape(cycle_size, local_count, capacity, width)
    gate_part = jnp.einsum(
        "nesd,edf->nesf", by_source, expert_gate, preferred_element_type=jnp.float32
    )
    up_part = jnp.einsum("nesd,edf->nesf", by_source, expert_up, preferred_element_type=jnp.float32)
    hidden = (jax.nn.silu(gate_part) * up_part).astype(jnp.bfloat16)
    produced = jnp.einsum(
        "nesf,efd->nesd", hidden, expert_down, preferred_element_type=jnp.float32
    ).astype(jnp.bfloat16)
    returned = lax.all_to_all(
        produced.reshape(cycle_size * local_count, capacity, width),
        "ctx",
        split_axis=0,
        concat_axis=0,
        tiled=True,
    )
    gathered = returned.reshape(expert_total * capacity, width)[slot_target].reshape(
        row_count, route_count, width
    )
    mixture = jnp.zeros((row_count, width), jnp.float32)
    for route in range(route_count):
        mixture = mixture + gate_weights[:, route : route + 1] * gathered[:, route].astype(
            jnp.float32
        )
    return attended, (widened + mixture).astype(jnp.bfloat16)


def slot_capacity(row_count, route_count, expert_total):
    return max(2, row_count * route_count * 9 // (8 * expert_total))


def shards(
    queries,
    keys,
    values,
    kv_lengths,
    stream,
    out_weight,
    routes,
    gate_weights,
    expert_gate,
    expert_up,
    expert_down,
):
    rows = queries.shape[0]
    devices = lax.axis_size("ctx")
    local_count = expert_gate.shape[0]
    capacity = slot_capacity(rows, routes.shape[1], local_count * devices)
    crowded = local_count == 1 and 4 * capacity > rows and devices % (4 * CORES) == 0
    crowded = crowded and out_weight.shape[0] == HD
    layer = ring_layer if crowded else slot_layer
    return layer(
        queries,
        keys,
        values,
        kv_lengths,
        stream,
        out_weight,
        routes,
        gate_weights,
        (expert_gate, expert_up, expert_down),
    )


def solution(mesh):
    return jax.shard_map(
        shards,
        mesh=mesh,
        in_specs=(
            P(("groups", "ctx"), None),
            P(("groups", "ctx"), None),
            P(("groups", "ctx"), None),
            P(("groups", "ctx")),
            P(("groups", "ctx"), None),
            P("ctx", None),
            P(("groups", "ctx"), None),
            P(("groups", "ctx"), None),
            P("ctx", None, None),
            P("ctx", None, None),
            P("ctx", None, None),
        ),
        out_specs=(P(("groups", "ctx"), None), P(("groups", "ctx"), None)),
        check_vma=False,
    )
```

profile of v0, /device:TPU:0, one launch (start us, length us, event | category | flops | bytes accessed | tf_op | source)
XLA Modules:
  0.0 203.7 jit_solution(14503711611938516786)
XLA Ops:
  0.6 3.1 %collective-permute-start.1 = (bf16[128,2048]{1,0:T(8,128)(2,1)}, bf16[128,2048]{1,0:T(8,128)(2,1)S(1)}, u32[]{:S(2)}, u32[]{:S(2)}) collective-permute-start(bf16[128,2048]{1,0:T(8,128)(2,1)} %refs_0_.1), channel_id=1, source_target_pairs={{0,4},{1,5},{4,8},{5,9},{8,12},{9,13},{12,14},{13,15},{14,10},{15,... | collective-permute-start | bytes 1572872 | tf_op jit(solution)/shard_map/ppermute | solution.py:274
  6.4 3.9 %collective-permute-start = (bf16[256,512]{1,0:T(8,128)(2,1)S(1)}, bf16[256,512]{1,0:T(8,128)(2,1)S(1)}, u32[]{:S(2)}, u32[]{:S(2)}) collective-permute-start(bf16[256,512]{1,0:T(8,128)(2,1)S(1)} %pad_maximum_fusion.2.refs_0_.refs_8_), channel_id=1, source_target_pairs={{0,4},{1,5},{2,6},{3,7},{4,8},{5,9},{6,10},{7,11},{8,12},{9,13},{1... | collective-permute-start | bytes 786440 | tf_op jit(solution)/shard_map/ppermute | solution.py:21
  11.1 9.7 %collective-permute-done.refs_1_.refs_9_ = bf16[256,512]{1,0:T(8,128)(2,1)S(1)} collective-permute-done((bf16[256,512]{1,0:T(8,128)(2,1)S(1)}, bf16[256,512]{1,0:T(8,128)(2,1)S(1)}, u32[]{:S(2)}, u32[]{:S(2)}) %collective-permute-start) | collective-permute-done | bytes 262176 | tf_op jit(solution)/shard_map/ppermute | solution.py:21
  20.8 2.5 %collective-permute-start.5 = (bf16[128,2048]{1,0:T(8,128)(2,1)S(1)}, bf16[128,2048]{1,0:T(8,128)(2,1)S(1)}, u32[]{:S(2)}, u32[]{:S(2)}) collective-permute-start(bf16[128,2048]{1,0:T(8,128)(2,1)S(1)} %collective-permute-done.1.refs_1_), channel_id=1, source_target_pairs={{0,4},{1,5},{4,8},{5,9},{8,12},{9,13},{12,14},{13,15},{14,10},{15,... | collective-permute-start | bytes 1572872 | tf_op jit(solution)/shard_map/ppermute | solution.py:274
  23.3 1.7 broadcast_select_fusion.2
  25.0 1.8 collective-permute-start.4
  26.7 3.9 %collective-permute-start.3 = (bf16[256,512]{1,0:T(8,128)(2,1)S(1)}, bf16[256,512]{1,0:T(8,128)(2,1)S(1)}, u32[]{:S(2)}, u32[]{:S(2)}) collective-permute-start(bf16[256,512]{1,0:T(8,128)(2,1)S(1)} %collective-permute-done.refs_1_.refs_9_), channel_id=1, source_target_pairs={{0,4},{1,5},{2,6},{3,7},{4,8},{5,9},{6,10},{7,11},{8,12},{9,13},{1... | collective-permute-start | bytes 786440 | tf_op jit(solution)/shard_map/ppermute | solution.py:21
  31.2 4.0 %all-to-all-start = ((f32[16,2,128]{2,1,0:T(2,128)}), f32[16,2,128]{2,1,0:T(2,128)S(1)}, u32[]{:S(2)}, u32[]{:S(2)}) async-start(f32[16,2,128]{2,1,0:T(2,128)} %copy.17), calls=%async_computation | async-start | bytes 32768 | tf_op jit(solution)/shard_map/all_to_all | solution.py:313
  35.6 6.1 %all-to-all-done = f32[16,2,128]{2,1,0:T(2,128)S(1)} async-done(((f32[16,2,128]{2,1,0:T(2,128)}), f32[16,2,128]{2,1,0:T(2,128)S(1)}, u32[]{:S(2)}, u32[]{:S(2)}) %all-to-all-start) | async-done | bytes 16416 | tf_op jit(solution)/shard_map/all_to_all | solution.py:313
  41.7 1.2 broadcast_select_fusion
  44.4 6.5 %collective-permute-done.9.refs_3_.refs_11_ = bf16[256,512]{1,0:T(8,128)(2,1)S(1)} collective-permute-done((bf16[256,512]{1,0:T(8,128)(2,1)S(1)}, bf16[256,512]{1,0:T(8,128)(2,1)S(1)}, u32[]{:S(2)}, u32[]{:S(2)}) %collective-permute-start.9) | collective-permute-done | bytes 262176 | tf_op jit(solution)/shard_map/ppermute | solution.py:321
  50.9 1.2 collective-permute-start.7
  53.0 10.7 %collective-permute-done.7.refs_5_ = bf16[128,2048]{1,0:T(8,128)(2,1)S(1)} collective-permute-done((bf16[128,2048]{1,0:T(8,128)(2,1)S(1)}, bf16[128,2048]{1,0:T(8,128)(2,1)S(1)}, u32[]{:S(2)}, u32[]{:S(2)}) %collective-permute-start.7) | collective-permute-done | bytes 524320 | tf_op jit(solution)/shard_map/ppermute | solution.py:274
  65.5 1.5 collective-permute-done.13.refs_7_.refs_15_
  67.0 2.1 %collective-permute-start.15 = (bf16[128,2048]{1,0:T(8,128)(2,1)}, bf16[128,2048]{1,0:T(8,128)(2,1)}, u32[]{:S(2)}, u32[]{:S(2)}) collective-permute-start(bf16[128,2048]{1,0:T(8,128)(2,1)} %copy-done.16), channel_id=1, source_target_pairs={{0,4},{1,5},{4,8},{5,9},{8,12},{9,13},{12,14},{13,15},{14,10},{15,... | collective-permute-start | bytes 1572872 | tf_op jit(solution)/shard_map/ppermute | solution.py:274
  69.9 1.0 copy-done.10
  70.9 11.8 %attend.1 = (bf16[128,2048]{1,0:T(8,128)(2,1)}, bf16[128,1024]{1,0:T(8,128)(2,1)S(1)}, bf16[128,1024]{1,0:T(8,128)(2,1)S(1)}) custom-call(s32[8]{0:T(128)S(1)} %compare_convert_fusion.length_ref, s32[1]{0:T(128)} %bitcast.core_ref, bf16[128,2048]{1,0:T(8,128)(2,1)S(1)} %copy-done.10, bf16[256,512]{1,0:T(8,128)(2,1)S(1)} %pad_maximum_fusion.2.refs_0_.refs_8_, ...), custom_call_target="tpu_custom_call" | custom-call | flops 2147483648 | bytes 3145728 | tf_op jit(solution)/shard_map/attend/pallas_call | solution.py:98
  82.8 1.5 collective-permute-done.14.got_ref
  85.0 1.0 copy-done.4
  87.0 4.8 %project.1 = (f32[128,2048]{1,0:T(8,128)S(1)}, f32[128,2048]{1,0:T(8,128)S(1)}) custom-call(s32[8]{0:T(128)S(1)} %get-tuple-element.111.order_ref, bf16[128,1024]{1,0:T(8,128)(2,1)S(1)} %get-tuple-element.75.mine_ref, bf16[128,1024]{1,0:T(8,128)(2,1)S(1)} %copy-done.9, bf16[128,2048]{1,0:T(8,128)(2,1)S(1)} %copy-done.4, bf16[128,2048]{1,0:T(8,128)(2,1)} %copy-done.12, ...), custom_call_target="tpu_custom_call" | custom-call | flops 1073741824 | bytes 6291456 | tf_op jit(solution)/shard_map/project/pallas_call | solution.py:206
  92.1 2.4 %collective-permute-done.16.got_ref = f32[128,2048]{1,0:T(8,128)S(1)} collective-permute-done((f32[128,2048]{1,0:T(8,128)S(1)}, f32[128,2048]{1,0:T(8,128)S(1)}, u32[]{:S(2)}, u32[]{:S(2)}) %collective-permute-start.16) | collective-permute-done | bytes 1048608 | tf_op jit(solution)/shard_map/ppermute | solution.py:277
  94.5 1.0 copy-done.5
  95.6 1.8 add_norm.1
  98.2 1.7 collective-permute-start.17
  100.3 1.1 copy.19
  102.3 1.9 copy-done.1
  104.2 1.9 copy-done.3
  106.1 6.8 %experts.5 = bf16[128,2048]{1,0:T(8,128)(2,1)S(1)} custom-call(bf16[128,2048]{1,0:T(8,128)(2,1)} %get-tuple-element.82.refs_0_, f32[128,2]{1,0:T(8,128)S(1)} %get-tuple-element.113.refs_1_, bf16[1,2048,768]{2,1,0:T(8,128)(2,1)S(1)} %copy-done, bf16[1,2048,768]{2,1,0:T(8,128)(2,1)S(1)} %copy-done.1, bf16[1,768,2048]{2,1,0:T(8,128)(2,1)S(1)} %copy-done.3, ...), custom_call_target="tpu_custom_call" | custom-call | flops 2415919104 | bytes 19922944 | tf_op jit(solution)/shard_map/experts/pallas_call | solution.py:153
  112.9 1.1 collective-permute-done.18.refs_1_
  113.9 1.1 collective-permute-start.22
  116.0 9.1 %experts.6 = (bf16[128,2048]{1,0:T(8,128)(2,1)S(1)}, bf16[128,2048]{1,0:T(8,128)(2,1)S(1)}) custom-call(bf16[128,2048]{1,0:T(8,128)(2,1)} %collective-permute-done.17.refs_0_, bf16[128,2048]{1,0:T(8,128)(2,1)} %collective-permute-done.18.refs_1_, f32[256,2]{1,0:T(8,128)S(1)} %bitcast.18, bf16[1,2048,768]{2,1,0:T(8,128)(2,1)S(1)} %copy-done, ...), custom_call_target="tpu_custom_call" | custom-call | flops 4831838208 | bytes 20971520 | tf_op jit(solution)/shard_map/experts/pallas_call | solution.py:153
  125.1 1.8 collective-permute-done.22.refs_0_
  128.0 1.1 collective-permute-start.24
  130.0 8.8 %experts.7 = (bf16[128,2048]{1,0:T(8,128)(2,1)S(1)}, bf16[128,2048]{1,0:T(8,128)(2,1)S(1)}) custom-call(bf16[128,2048]{1,0:T(8,128)(2,1)S(1)} %collective-permute-done.22.refs_0_, bf16[128,2048]{1,0:T(8,128)(2,1)S(1)} %collective-permute-done.23.refs_1_, f32[256,2]{1,0:T(8,128)S(1)} %bitcast.17, bf16[1,2048,768]{2,1,0:T(8,128)(2,1)S(1)} %copy-done, ...), custom_call_target="tpu_custom_call" | custom-call | flops 4831838208 | bytes 20971520 | tf_op jit(solution)/shard_map/experts/pallas_call | solution.py:153
  138.8 1.1 collective-permute-done.24.refs_0_
  139.9 1.2 collective-permute-done.25.refs_1_
  141.7 1.5 collective-permute-start.27
  143.2 8.8 %experts.8 = (bf16[128,2048]{1,0:T(8,128)(2,1)S(1)}, bf16[128,2048]{1,0:T(8,128)(2,1)S(1)}) custom-call(bf16[128,2048]{1,0:T(8,128)(2,1)S(1)} %collective-permute-done.24.refs_0_, bf16[128,2048]{1,0:T(8,128)(2,1)S(1)} %collective-permute-done.25.refs_1_, f32[256,2]{1,0:T(8,128)S(1)} %bitcast.16, bf16[1,2048,768]{2,1,0:T(8,128)(2,1)S(1)} %copy-done, ...), custom_call_target="tpu_custom_call" | custom-call | flops 4831838208 | bytes 20971520 | tf_op jit(solution)/shard_map/experts/pallas_call | solution.py:153
  152.1 6.5 %experts.9 = (bf16[64,2048]{1,0:T(8,128)(2,1)S(1)}, bf16[64,2048]{1,0:T(8,128)(2,1)S(1)}) custom-call(bf16[64,2048]{1,0:T(8,128)(2,1)S(1)} %collective-permute-done.26.refs_0_, bf16[64,2048]{1,0:T(8,128)(2,1)S(1)} %collective-permute-done.27.refs_1_, f32[128,2]{1,0:T(8,128)S(1)} %get-tuple-element.112.refs_2_, bf16[1,2048,768]{2,1,0:T(8,128)(2,1)S(1)} %copy-done, ...), custom_call_target="tpu_custom_call" | custom-call | flops 2415919104 | bytes 19922944 | tf_op jit(solution)/shard_map/experts/pallas_call | solution.py:153
  159.2 1.5 collective-permute-start.32
  160.7 5.9 %collective-permute-done.28 = bf16[64,2048]{1,0:T(8,128)(2,1)S(1)} collective-permute-done((bf16[64,2048]{1,0:T(8,128)(2,1)S(1)}, bf16[64,2048]{1,0:T(8,128)(2,1)S(1)}, u32[]{:S(2)}, u32[]{:S(2)}) %collective-permute-start.28) | collective-permute-done | bytes 262176 | tf_op jit(solution)/shard_map/ppermute | solution.py:274
  167.9 1.2 collective-permute-start.33
  169.1 9.6 %collective-permute-done.29 = bf16[128,2048]{1,0:T(8,128)(2,1)S(1)} collective-permute-done((bf16[128,2048]{1,0:T(8,128)(2,1)S(1)}, bf16[128,2048]{1,0:T(8,128)(2,1)S(1)}, u32[]{:S(2)}, u32[]{:S(2)}) %collective-permute-start.29) | collective-permute-done | bytes 524320 | tf_op jit(solution)/shard_map/ppermute | solution.py:274
  181.2 10.5 %collective-permute-done.30 = bf16[128,2048]{1,0:T(8,128)(2,1)S(1)} collective-permute-done((bf16[128,2048]{1,0:T(8,128)(2,1)S(1)}, bf16[128,2048]{1,0:T(8,128)(2,1)S(1)}, u32[]{:S(2)}, u32[]{:S(2)}) %collective-permute-start.30) | collective-permute-done | bytes 524320 | tf_op jit(solution)/shard_map/ppermute | solution.py:274
  191.8 1.4 collective-permute-start.31
  194.1 7.0 %collective-permute-done.31 = bf16[128,2048]{1,0:T(8,128)(2,1)S(1)} collective-permute-done((bf16[128,2048]{1,0:T(8,128)(2,1)S(1)}, bf16[128,2048]{1,0:T(8,128)(2,1)S(1)}, u32[]{:S(2)}, u32[]{:S(2)}) %collective-permute-start.31) | collective-permute-done | bytes 524320 | tf_op jit(solution)/shard_map/ppermute | solution.py:274
  201.1 1.5 collective-permute-done.35
  202.6 1.1 add_convert_fusion
  (102 shorter events, 21.6 us)
Async XLA Ops:
  0.6 20.1 %collective-permute-start.1 = (bf16[128,2048]{1,0:T(8,128)(2,1)}, bf16[128,2048]{1,0:T(8,128)(2,1)S(1)}, u32[]{:S(2)}, u32[]{:S(2)}) collective-permute-start(bf16[128,2048]{1,0:T(8,128)(2,1)} %refs_0_.1), channel_id=1, source_target_pairs={{0,4},{1,5},{4,8},{5,9},{8,12},{9,13},{12,14},{13,15},{14,10},{15,... | collective-permute-start | bytes 1572872 | tf_op jit(solution)/shard_map/ppermute | solution.py:274
  3.7 17.0 %collective-permute-start.2 = (bf16[128,2048]{1,0:T(8,128)(2,1)}, bf16[128,2048]{1,0:T(8,128)(2,1)S(1)}, u32[]{:S(2)}, u32[]{:S(2)}) collective-permute-start(bf16[128,2048]{1,0:T(8,128)(2,1)} %refs_0_.1), channel_id=1, source_target_pairs={{0,2},{1,3},{4,0},{5,1},{8,4},{9,5},{12,8},{13,9},{14,12},{15,13},... | collective-permute-start | bytes 1572872 | tf_op jit(solution)/shard_map/ppermute | solution.py:274
  6.4 14.4 %collective-permute-start = (bf16[256,512]{1,0:T(8,128)(2,1)S(1)}, bf16[256,512]{1,0:T(8,128)(2,1)S(1)}, u32[]{:S(2)}, u32[]{:S(2)}) collective-permute-start(bf16[256,512]{1,0:T(8,128)(2,1)S(1)} %pad_maximum_fusion.2.refs_0_.refs_8_), channel_id=1, source_target_pairs={{0,4},{1,5},{2,6},{3,7},{4,8},{5,9},{6,10},{7,11},{8,12},{9,13},{1... | collective-permute-start | bytes 786440 | tf_op jit(solution)/shard_map/ppermute | solution.py:21
  20.7 22.1 %copy-start.12 = (bf16[128,2048]{1,0:T(8,128)(2,1)}, bf16[128,2048]{1,0:T(8,128)(2,1)S(1)}, u32[]{:S(2)}) copy-start(bf16[128,2048]{1,0:T(8,128)(2,1)S(1)} %collective-permute-done.1.refs_1_) | copy-start | bytes 1572868
  20.8 32.2 %copy-start.13 = (bf16[128,2048]{1,0:T(8,128)(2,1)}, bf16[128,2048]{1,0:T(8,128)(2,1)S(1)}, u32[]{:S(2)}) copy-start(bf16[128,2048]{1,0:T(8,128)(2,1)S(1)} %collective-permute-done.2.refs_2_) | copy-start | bytes 1572868
  20.8 20.9 %collective-permute-start.5 = (bf16[128,2048]{1,0:T(8,128)(2,1)S(1)}, bf16[128,2048]{1,0:T(8,128)(2,1)S(1)}, u32[]{:S(2)}, u32[]{:S(2)}) collective-permute-start(bf16[128,2048]{1,0:T(8,128)(2,1)S(1)} %collective-permute-done.1.refs_1_), channel_id=1, source_target_pairs={{0,4},{1,5},{4,8},{5,9},{8,12},{9,13},{12,14},{13,15},{14,10},{15,... | collective-permute-start | bytes 1572872 | tf_op jit(solution)/shard_map/ppermute | solution.py:274
  23.3 18.4 %collective-permute-start.6 = (bf16[128,2048]{1,0:T(8,128)(2,1)S(1)}, bf16[128,2048]{1,0:T(8,128)(2,1)S(1)}, u32[]{:S(2)}, u32[]{:S(2)}) collective-permute-start(bf16[128,2048]{1,0:T(8,128)(2,1)S(1)} %collective-permute-done.2.refs_2_), channel_id=1, source_target_pairs={{0,2},{1,3},{4,0},{5,1},{8,4},{9,5},{12,8},{13,9},{14,12},{15,13},... | collective-permute-start | bytes 1572872 | tf_op jit(solution)/shard_map/ppermute | solution.py:274
  25.0 16.7 %collective-permute-start.4 = (bf16[256,512]{1,0:T(8,128)(2,1)}, bf16[256,512]{1,0:T(8,128)(2,1)S(1)}, u32[]{:S(2)}, u32[]{:S(2)}) collective-permute-start(bf16[256,512]{1,0:T(8,128)(2,1)} %broadcast_select_fusion.2), channel_id=1, source_target_pairs={{0,2},{1,3},{2,0},{3,1},{4,6},{5,7},{6,4},{7,5},{8,10},{9,11},{10,... | collective-permute-start | bytes 786440 | tf_op jit(solution)/shard_map/ppermute | solution.py:315
  26.7 14.9 %collective-permute-start.3 = (bf16[256,512]{1,0:T(8,128)(2,1)S(1)}, bf16[256,512]{1,0:T(8,128)(2,1)S(1)}, u32[]{:S(2)}, u32[]{:S(2)}) collective-permute-start(bf16[256,512]{1,0:T(8,128)(2,1)S(1)} %collective-permute-done.refs_1_.refs_9_), channel_id=1, source_target_pairs={{0,4},{1,5},{2,6},{3,7},{4,8},{5,9},{6,10},{7,11},{8,12},{9,13},{1... | collective-permute-start | bytes 786440 | tf_op jit(solution)/shard_map/ppermute | solution.py:21
  31.2 10.5 %all-to-all-start = ((f32[16,2,128]{2,1,0:T(2,128)}), f32[16,2,128]{2,1,0:T(2,128)S(1)}, u32[]{:S(2)}, u32[]{:S(2)}) async-start(f32[16,2,128]{2,1,0:T(2,128)} %copy.17), calls=%async_computation | async-start | bytes 32768 | tf_op jit(solution)/shard_map/all_to_all | solution.py:313
  35.2 8.7 %collective-permute-start.11 = (bf16[256,512]{1,0:T(8,128)(2,1)S(1)}, bf16[256,512]{1,0:T(8,128)(2,1)S(1)}, u32[]{:S(2)}, u32[]{:S(2)}) collective-permute-start(bf16[256,512]{1,0:T(8,128)(2,1)S(1)} %collective-permute-done.refs_1_.refs_9_), channel_id=1, source_target_pairs={{0,1},{1,0},{2,3},{3,2},{4,5},{5,4},{6,7},{7,6},{8,9},{9,8},{10,11... | collective-permute-start | bytes 786440 | tf_op jit(solution)/shard_map/ppermute | solution.py:277
  41.7 22.0 %copy-start.14 = (bf16[128,2048]{1,0:T(8,128)(2,1)}, bf16[128,2048]{1,0:T(8,128)(2,1)S(1)}, u32[]{:S(2)}) copy-start(bf16[128,2048]{1,0:T(8,128)(2,1)S(1)} %collective-permute-done.5.refs_3_) | copy-start | bytes 1572868
  41.7 28.1 %copy-start.15 = (bf16[128,2048]{1,0:T(8,128)(2,1)}, bf16[128,2048]{1,0:T(8,128)(2,1)S(1)}, u32[]{:S(2)}) copy-start(bf16[128,2048]{1,0:T(8,128)(2,1)S(1)} %collective-permute-done.6.refs_4_) | copy-start | bytes 1572868
  42.9 8.0 %collective-permute-start.9 = (bf16[256,512]{1,0:T(8,128)(2,1)S(1)}, bf16[256,512]{1,0:T(8,128)(2,1)S(1)}, u32[]{:S(2)}, u32[]{:S(2)}) collective-permute-start(bf16[256,512]{1,0:T(8,128)(2,1)S(1)} %get-tuple-element.118), channel_id=1, source_target_pairs={{0,2},{1,3},{2,0},{3,1},{4,6},{5,7},{6,4},{7,5},{8,10},{9,11},{10,... | collective-permute-start | bytes 786440 | tf_op jit(solution)/shard_map/ppermute | solution.py:321
  43.4 8.7 %collective-permute-start.10 = (bf16[256,512]{1,0:T(8,128)(2,1)S(1)}, bf16[256,512]{1,0:T(8,128)(2,1)S(1)}, u32[]{:S(2)}, u32[]{:S(2)}) collective-permute-start(bf16[256,512]{1,0:T(8,128)(2,1)S(1)} %get-tuple-element.117), channel_id=1, source_target_pairs={{0,1},{1,0},{2,3},{3,2},{4,5},{5,4},{6,7},{7,6},{8,9},{9,8},{10,11... | collective-permute-start | bytes 786440 | tf_op jit(solution)/shard_map/ppermute | solution.py:277
  43.4 58.8 %collective-permute-start.19 = (bf16[1,2048,768]{2,1,0:T(8,128)(2,1)}, bf16[1,2048,768]{2,1,0:T(8,128)(2,1)}, u32[]{:S(2)}, u32[]{:S(2)}) collective-permute-start(bf16[1,2048,768]{2,1,0:T(8,128)(2,1)} %refs_3_.9), channel_id=1, source_target_pairs={{0,1},{1,0},{2,3},{3,2},{4,5},{5,4},{6,7},{7,6},{8,9},{9,8},{10,11... | collective-permute-start | bytes 9437192 | tf_op jit(solution)/shard_map/ppermute | solution.py:277
  43.9 58.3 %collective-permute-start.20 = (bf16[1,2048,768]{2,1,0:T(8,128)(2,1)}, bf16[1,2048,768]{2,1,0:T(8,128)(2,1)}, u32[]{:S(2)}, u32[]{:S(2)}) collective-permute-start(bf16[1,2048,768]{2,1,0:T(8,128)(2,1)} %refs_4_.9), channel_id=1, source_target_pairs={{0,1},{1,0},{2,3},{3,2},{4,5},{5,4},{6,7},{7,6},{8,9},{9,8},{10,11... | collective-permute-start | bytes 9437192 | tf_op jit(solution)/shard_map/ppermute | solution.py:277
  43.9 58.3 %collective-permute-start.21 = (bf16[1,768,2048]{2,1,0:T(8,128)(2,1)}, bf16[1,768,2048]{2,1,0:T(8,128)(2,1)}, u32[]{:S(2)}, u32[]{:S(2)}) collective-permute-start(bf16[1,768,2048]{2,1,0:T(8,128)(2,1)} %refs_5_.7), channel_id=1, source_target_pairs={{0,1},{1,0},{2,3},{3,2},{4,5},{5,4},{6,7},{7,6},{8,9},{9,8},{10,11... | collective-permute-start | bytes 9437192 | tf_op jit(solution)/shard_map/ppermute | solution.py:277
  50.9 12.7 %collective-permute-start.7 = (bf16[128,2048]{1,0:T(8,128)(2,1)S(1)}, bf16[128,2048]{1,0:T(8,128)(2,1)S(1)}, u32[]{:S(2)}, u32[]{:S(2)}) collective-permute-start(bf16[128,2048]{1,0:T(8,128)(2,1)S(1)} %collective-permute-done.5.refs_3_), channel_id=1, source_target_pairs={{0,4},{1,5},{4,8},{5,9},{8,12},{9,13},{12,14},{13,15},{14,10},{15,... | collective-permute-start | bytes 1572872 | tf_op jit(solution)/shard_map/ppermute | solution.py:274
  52.2 12.5 %collective-permute-start.8 = (bf16[128,2048]{1,0:T(8,128)(2,1)S(1)}, bf16[128,2048]{1,0:T(8,128)(2,1)S(1)}, u32[]{:S(2)}, u32[]{:S(2)}) collective-permute-start(bf16[128,2048]{1,0:T(8,128)(2,1)S(1)} %collective-permute-done.6.refs_4_), channel_id=1, source_target_pairs={{0,2},{1,3},{4,0},{5,1},{8,4},{9,5},{12,8},{13,9},{14,12},{15,13},... | collective-permute-start | bytes 1572872 | tf_op jit(solution)/shard_map/ppermute | solution.py:274
  63.6 1.9 collective-permute-start.12
  65.5 1.5 collective-permute-start.13
  67.0 17.9 %collective-permute-start.15 = (bf16[128,2048]{1,0:T(8,128)(2,1)}, bf16[128,2048]{1,0:T(8,128)(2,1)}, u32[]{:S(2)}, u32[]{:S(2)}) collective-permute-start(bf16[128,2048]{1,0:T(8,128)(2,1)} %copy-done.16), channel_id=1, source_target_pairs={{0,4},{1,5},{4,8},{5,9},{8,12},{9,13},{12,14},{13,15},{14,10},{15,... | collective-permute-start | bytes 1572872 | tf_op jit(solution)/shard_map/ppermute | solution.py:274
  70.9 11.8 %copy-start.18 = (s32[8]{0:T(128)S(1)}, s32[8]{0:T(128)}, u32[]{:S(2)}) copy-start(s32[8]{0:T(128)} %constant.79.clone) | copy-start | bytes 100
  82.7 1.5 collective-permute-start.14
  87.0 15.3 %copy-start = (bf16[1,2048,768]{2,1,0:T(8,128)(2,1)S(1)}, bf16[1,2048,768]{2,1,0:T(8,128)(2,1)}, u32[]{:S(2)}) copy-start(bf16[1,2048,768]{2,1,0:T(8,128)(2,1)} %refs_3_.9) | copy-start | bytes 9437188
  91.8 2.7 %collective-permute-start.16 = (f32[128,2048]{1,0:T(8,128)S(1)}, f32[128,2048]{1,0:T(8,128)S(1)}, u32[]{:S(2)}, u32[]{:S(2)}) collective-permute-start(f32[128,2048]{1,0:T(8,128)S(1)} %get-tuple-element.80), channel_id=1, source_target_pairs={{0,1},{1,0},{2,3},{3,2},{4,5},{5,4},{6,7},{7,6},{8,9},{9,8},{10,11... | collective-permute-start | bytes 3145736 | tf_op jit(solution)/shard_map/ppermute | solution.py:277
  98.2 14.7 %collective-permute-start.17 = (bf16[128,2048]{1,0:T(8,128)(2,1)}, bf16[128,2048]{1,0:T(8,128)(2,1)}, u32[]{:S(2)}, u32[]{:S(2)}) collective-permute-start(bf16[128,2048]{1,0:T(8,128)(2,1)} %get-tuple-element.82.refs_0_), channel_id=1, source_target_pairs={{0,4},{1,5},{4,8},{5,9},{8,12},{9,13},{12,14},{13,15},{14,10},{15,... | collective-permute-start | bytes 1572872 | tf_op jit(solution)/shard_map/ppermute | solution.py:274
  99.9 14.0 %collective-permute-start.18 = (bf16[128,2048]{1,0:T(8,128)(2,1)}, bf16[128,2048]{1,0:T(8,128)(2,1)}, u32[]{:S(2)}, u32[]{:S(2)}) collective-permute-start(bf16[128,2048]{1,0:T(8,128)(2,1)} %get-tuple-element.82.refs_0_), channel_id=1, source_target_pairs={{0,2},{1,3},{4,0},{5,1},{8,4},{9,5},{12,8},{13,9},{14,12},{15,13},... | collective-permute-start | bytes 1572872 | tf_op jit(solution)/shard_map/ppermute | solution.py:274
  102.3 1.9 copy-start.1
  104.2 1.9 copy-start.3
  106.1 9.9 %copy-start.11 = (f32[8,2,128]{1,2,0:T(8,128)S(1)}, f32[8,2,128]{1,2,0:T(8,128)}, u32[]{:S(2)}) copy-start(f32[8,2,128]{1,2,0:T(8,128)} %copy.19) | copy-start | bytes 24580
  106.1 9.9 %copy-start.2 = (bf16[1,2048,768]{2,1,0:T(8,128)(2,1)S(1)}, bf16[1,2048,768]{2,1,0:T(8,128)(2,1)}, u32[]{:S(2)}) copy-start(bf16[1,2048,768]{2,1,0:T(8,128)(2,1)} %refs_4_.9) | copy-start | bytes 9437188
  113.9 13.0 %collective-permute-start.22 = (bf16[128,2048]{1,0:T(8,128)(2,1)}, bf16[128,2048]{1,0:T(8,128)(2,1)S(1)}, u32[]{:S(2)}, u32[]{:S(2)}) collective-permute-start(bf16[128,2048]{1,0:T(8,128)(2,1)} %collective-permute-done.17.refs_0_), channel_id=1, source_target_pairs={{0,4},{1,5},{4,8},{5,9},{8,12},{9,13},{12,14},{13,15},{14,10},{15,... | collective-permute-start | bytes 1572872 | tf_op jit(solution)/shard_map/ppermute | solution.py:274
  115.0 13.0 %collective-permute-start.23 = (bf16[128,2048]{1,0:T(8,128)(2,1)}, bf16[128,2048]{1,0:T(8,128)(2,1)S(1)}, u32[]{:S(2)}, u32[]{:S(2)}) collective-permute-start(bf16[128,2048]{1,0:T(8,128)(2,1)} %collective-permute-done.18.refs_1_), channel_id=1, source_target_pairs={{0,2},{1,3},{4,0},{5,1},{8,4},{9,5},{12,8},{13,9},{14,12},{15,13},... | collective-permute-start | bytes 1572872 | tf_op jit(solution)/shard_map/ppermute | solution.py:274
  128.0 11.9 %collective-permute-start.24 = (bf16[128,2048]{1,0:T(8,128)(2,1)S(1)}, bf16[128,2048]{1,0:T(8,128)(2,1)S(1)}, u32[]{:S(2)}, u32[]{:S(2)}) collective-permute-start(bf16[128,2048]{1,0:T(8,128)(2,1)S(1)} %collective-permute-done.22.refs_0_), channel_id=1, source_target_pairs={{0,4},{1,5},{4,8},{5,9},{8,12},{9,13},{12,14},{13,15},{14,10},{15,... | collective-permute-start | bytes 1572872 | tf_op jit(solution)/shard_map/ppermute | solution.py:274
  129.1 12.0 %collective-permute-start.25 = (bf16[128,2048]{1,0:T(8,128)(2,1)S(1)}, bf16[128,2048]{1,0:T(8,128)(2,1)S(1)}, u32[]{:S(2)}, u32[]{:S(2)}) collective-permute-start(bf16[128,2048]{1,0:T(8,128)(2,1)S(1)} %collective-permute-done.23.refs_1_), channel_id=1, source_target_pairs={{0,2},{1,3},{4,0},{5,1},{8,4},{9,5},{12,8},{13,9},{14,12},{15,13},... | collective-permute-start | bytes 1572872 | tf_op jit(solution)/shard_map/ppermute | solution.py:274
  141.1 11.0 %collective-permute-start.26 = (bf16[64,2048]{1,0:T(8,128)(2,1)S(1)}, bf16[64,2048]{1,0:T(8,128)(2,1)S(1)}, u32[]{:S(2)}, u32[]{:S(2)}) collective-permute-start(bf16[64,2048]{1,0:T(8,128)(2,1)S(1)} %slice.54), channel_id=1, source_target_pairs={{0,4},{1,5},{4,8},{5,9},{8,12},{9,13},{12,14},{13,15},{14,10},{15,... | collective-permute-start | bytes 786440 | tf_op jit(solution)/shard_map/ppermute | solution.py:274
  141.7 10.3 %collective-permute-start.27 = (bf16[64,2048]{1,0:T(8,128)(2,1)S(1)}, bf16[64,2048]{1,0:T(8,128)(2,1)S(1)}, u32[]{:S(2)}, u32[]{:S(2)}) collective-permute-start(bf16[64,2048]{1,0:T(8,128)(2,1)S(1)} %slice.55), channel_id=1, source_target_pairs={{0,2},{1,3},{4,0},{5,1},{8,4},{9,5},{12,8},{13,9},{14,12},{15,13},... | collective-permute-start | bytes 786440 | tf_op jit(solution)/shard_map/ppermute | solution.py:274
  158.6 8.1 %collective-permute-start.28 = (bf16[64,2048]{1,0:T(8,128)(2,1)S(1)}, bf16[64,2048]{1,0:T(8,128)(2,1)S(1)}, u32[]{:S(2)}, u32[]{:S(2)}) collective-permute-start(bf16[64,2048]{1,0:T(8,128)(2,1)S(1)} %get-tuple-element.102), channel_id=1, source_target_pairs={{0,2},{1,3},{4,0},{5,1},{8,4},{9,5},{12,8},{13,9},{14,12},{15,13},... | collective-permute-start | bytes 786440 | tf_op jit(solution)/shard_map/ppermute | solution.py:274
  159.2 8.5 %collective-permute-start.32 = (bf16[64,2048]{1,0:T(8,128)(2,1)S(1)}, bf16[64,2048]{1,0:T(8,128)(2,1)S(1)}, u32[]{:S(2)}, u32[]{:S(2)}) collective-permute-start(bf16[64,2048]{1,0:T(8,128)(2,1)S(1)} %get-tuple-element.107), channel_id=1, source_target_pairs={{0,4},{1,5},{4,8},{5,9},{8,12},{9,13},{12,14},{13,15},{14,10},{15,... | collective-permute-start | bytes 786440 | tf_op jit(solution)/shard_map/ppermute | solution.py:274
  166.7 12.0 %collective-permute-start.29 = (bf16[128,2048]{1,0:T(8,128)(2,1)S(1)}, bf16[128,2048]{1,0:T(8,128)(2,1)S(1)}, u32[]{:S(2)}, u32[]{:S(2)}) collective-permute-start(bf16[128,2048]{1,0:T(8,128)(2,1)S(1)} %pad_maximum_fusion), channel_id=1, source_target_pairs={{0,2},{1,3},{4,0},{5,1},{8,4},{9,5},{12,8},{13,9},{14,12},{15,13},... | collective-permute-start | bytes 1572872 | tf_op jit(solution)/shard_map/ppermute | solution.py:274
  167.8 34.7 %copy-start.7 = (bf16[128,2048]{1,0:T(8,128)(2,1)S(1)}, bf16[128,2048]{1,0:T(8,128)(2,1)}, u32[]{:S(2)}) copy-start(bf16[128,2048]{1,0:T(8,128)(2,1)} %copy-done.6) | copy-start | bytes 1572868
  167.9 12.2 %collective-permute-start.33 = (bf16[128,2048]{1,0:T(8,128)(2,1)S(1)}, bf16[128,2048]{1,0:T(8,128)(2,1)S(1)}, u32[]{:S(2)}, u32[]{:S(2)}) collective-permute-start(bf16[128,2048]{1,0:T(8,128)(2,1)S(1)} %pad_maximum_fusion.1), channel_id=1, source_target_pairs={{0,4},{1,5},{4,8},{5,9},{8,12},{9,13},{12,14},{13,15},{14,10},{15,... | collective-permute-start | bytes 1572872 | tf_op jit(solution)/shard_map/ppermute | solution.py:274
  178.8 12.9 %collective-permute-start.30 = (bf16[128,2048]{1,0:T(8,128)(2,1)S(1)}, bf16[128,2048]{1,0:T(8,128)(2,1)S(1)}, u32[]{:S(2)}, u32[]{:S(2)}) collective-permute-start(bf16[128,2048]{1,0:T(8,128)(2,1)S(1)} %add_convert_fusion.4), channel_id=1, source_target_pairs={{0,2},{1,3},{4,0},{5,1},{8,4},{9,5},{12,8},{13,9},{14,12},{15,13},... | collective-permute-start | bytes 1572872 | tf_op jit(solution)/shard_map/ppermute | solution.py:274
  180.2 13.1 %collective-permute-start.34 = (bf16[128,2048]{1,0:T(8,128)(2,1)S(1)}, bf16[128,2048]{1,0:T(8,128)(2,1)S(1)}, u32[]{:S(2)}, u32[]{:S(2)}) collective-permute-start(bf16[128,2048]{1,0:T(8,128)(2,1)S(1)} %add_convert_fusion.2), channel_id=1, source_target_pairs={{0,4},{1,5},{4,8},{5,9},{8,12},{9,13},{12,14},{13,15},{14,10},{15,... | collective-permute-start | bytes 1572872 | tf_op jit(solution)/shard_map/ppermute | solution.py:274
  191.8 9.2 %collective-permute-start.31 = (bf16[128,2048]{1,0:T(8,128)(2,1)S(1)}, bf16[128,2048]{1,0:T(8,128)(2,1)S(1)}, u32[]{:S(2)}, u32[]{:S(2)}) collective-permute-start(bf16[128,2048]{1,0:T(8,128)(2,1)S(1)} %add_convert_fusion.3), channel_id=1, source_target_pairs={{0,2},{1,3},{4,0},{5,1},{8,4},{9,5},{12,8},{13,9},{14,12},{15,13},... | collective-permute-start | bytes 1572872 | tf_op jit(solution)/shard_map/ppermute | solution.py:274
  193.3 9.2 %collective-permute-start.35 = (bf16[128,2048]{1,0:T(8,128)(2,1)S(1)}, bf16[128,2048]{1,0:T(8,128)(2,1)S(1)}, u32[]{:S(2)}, u32[]{:S(2)}) collective-permute-start(bf16[128,2048]{1,0:T(8,128)(2,1)S(1)} %add_convert_fusion.1), channel_id=1, source_target_pairs={{0,4},{1,5},{4,8},{5,9},{8,12},{9,13},{12,14},{13,15},{14,10},{15,... | collective-permute-start | bytes 1572872 | tf_op jit(solution)/shard_map/ppermute | solution.py:274
  (8 other events, 7.5 us)
where the time goes:
time: 204 us
  waiting for transfers between devices  80.4 us (39%)
  Pallas kernels  58.4 us (29%)
  starting transfers between devices  42.1 us (21%)
  local copies, waits for them, and re-layouts  12.9 us (6%)
  other arithmetic  8.19 us (4%)
    ppermute x23, waiting for transfers between devices, moved(): return lax.ppermute(block, 'ctx', route)  52.7 us
    pallas_call x5, Pallas kernels, run_experts(): pl.pallas_call(functools.partial(expert_kernel, count), in_specs=[held] *...  40 us
    ppermute x23, starting transfers between devices, moved(): return lax.ppermute(block, 'ctx', route)  26.5 us
    pallas_call x1, Pallas kernels, attend(): pl.pallas_call(functools.partial(attend_kernel, pair, len(windows)), grid...  11.8 us
    unnamed x38, local copies, waits for them, and re-layouts  10.2 us
    ppermute x2, waiting for transfers between devices, from_behind(): return lax.ppermute(block, axis, route)  9.68 us
    ppermute x2, starting transfers between devices, from_behind(): return lax.ppermute(block, axis, route)  7.8 us
    ppermute x1, waiting for transfers between devices, ring_layer(): lax.ppermute(jnp.where(side == 0, second, fourth), 'ctx', flip[1])  6.48 us
  transfers between devices with their start and end apart: 37, of which 20 were waited for; matrix products, arithmetic and copies ran while one was open for 5% of the time, Pallas kernels for 26%

commit v1 on v0

--- a/solution.py
+++ b/solution.py
@@ -124,17 +124,18 @@
     return window
 
 
-def expert_kernel(count, *refs):
+def expert_kernel(count, first, *refs):
     x_refs = refs[:count]
     factor_ref = refs[count]
     trios = (refs[count + 1 : count + 4], refs[count + 4 : count + 7])
     o_refs = refs[count + 7 :]
     x = jnp.concatenate([x_ref[...] for x_ref in x_refs], axis=0)
+    scale = factor_ref[first : first + x.shape[0], :]
     total = None
     for column, (gate_ref, up_ref, down_ref) in enumerate(trios):
         gate = jnp.dot(x, gate_ref[0], preferred_element_type=jnp.float32)
         up = jnp.dot(x, up_ref[0], preferred_element_type=jnp.float32)
-        hidden = gate / (1.0 + jnp.exp(-gate)) * up * factor_ref[:, column : column + 1]
+        hidden = gate / (1.0 + jnp.exp(-gate)) * up * scale[:, column : column + 1]
         part = jnp.dot(hidden.astype(jnp.bfloat16), down_ref[0], preferred_element_type=jnp.float32)
         total = part if total is None else total + part
     low = 0
@@ -144,14 +145,14 @@
         low = high
 
 
-def run_experts(blocks, factors, own, other):
+def run_experts(blocks, factors, first, own, other):
     width = blocks[0].shape[1]
     hidden = own[0].shape[2]
     rows = sum(block.shape[0] for block in blocks)
     count = len(blocks)
     held = pl.BlockSpec(memory_space=pltpu.VMEM)
     return pl.pallas_call(
-        functools.partial(expert_kernel, count),
+        functools.partial(expert_kernel, count, first),
         in_specs=[held] * (count + 7),
         out_specs=[held] * count,
         out_shape=[jax.ShapeDtypeStruct(block.shape, jnp.bfloat16) for block in blocks],
@@ -175,16 +176,18 @@
     return widened, normed
 
 
-def project_kernel(order_ref, mine_ref, got_ref, *refs):
-    *pieces, keep_ref, give_ref = refs
-    rows = mine_ref.shape[0]
-    total = None
+def project_kernel(count, sums, order_ref, *refs):
+    row_refs, refs = refs[:count], refs[count:]
+    sum_refs, refs = refs[:sums], refs[sums:]
+    pieces, o_refs = refs[:-count], refs[-count:]
+    rows = row_refs[0].shape[0]
+    total = jnp.concatenate([sum_ref[...] for sum_ref in sum_refs], axis=0) if sums else None
     for index in range(0, len(pieces), 2):
         columns = []
         for place in (index, index + 1):
             low = pl.multiple_of(order_ref[place] * HD, HD)
             columns.append(
-                jnp.concatenate([mine_ref[:, pl.ds(low, HD)], got_ref[:, pl.ds(low, HD)]], axis=0)
+                jnp.concatenate([row_ref[:, pl.ds(low, HD)] for row_ref in row_refs], axis=0)
             )
         part = jnp.dot(
             jnp.concatenate(columns, axis=1),
@@ -192,39 +195,59 @@
             preferred_element_type=jnp.float32,
         )
         total = part if total is None else total + part
-    keep_ref[...] = total[:rows]
-    give_ref[...] = total[rows:]
-
-
-def project_pieces(mine, got, pieces, order):
-    rows = mine.shape[0]
+    for i, o_ref in enumerate(o_refs):
+        o_ref[...] = total[i * rows : (i + 1) * rows].astype(o_ref.dtype)
+
+
+def project_pieces(blocks, pieces, order, sums=()):
+    rows = blocks[0].shape[0]
     width = pieces[0].shape[1]
     part = 512 if width % 512 == 0 else width
-    whole = pl.BlockSpec(mine.shape, lambda i, n: (0, 0))
+    whole = pl.BlockSpec(blocks[0].shape, lambda i, n: (0, 0))
     wide = pl.BlockSpec((rows, part), lambda i, n: (0, i))
     like = jax.ShapeDtypeStruct((rows, width), jnp.float32)
+    count = len(blocks)
     return pl.pallas_call(
-        project_kernel,
+        functools.partial(project_kernel, count, len(sums)),
         grid_spec=pltpu.PrefetchScalarGridSpec(
             num_scalar_prefetch=1,
             grid=(width // part,),
-            in_specs=[whole, whole]
+            in_specs=[whole] * count
+            + [wide] * len(sums)
             + [pl.BlockSpec((piece.shape[0], part), lambda i, n: (0, i)) for piece in pieces],
-            out_specs=[wide, wide],
+            out_specs=[wide] * count,
         ),
-        out_shape=[like, like],
+        out_shape=[like] * count,
         compiler_params=pltpu.CompilerParams(vmem_limit_bytes=20 * 1024 * 1024),
         cost_estimate=pl.CostEstimate(
-            flops=4 * rows * width * mine.shape[1],
+            flops=2 * count * rows * width * len(pieces) * HD,
             transcendentals=0,
-            bytes_accessed=2 * mine.shape[1] * width + 8 * rows * width,
+            bytes_accessed=2 * len(pieces) * HD * width + 4 * count * rows * width,
         ),
         name="project",
-    )(order, mine, got, *pieces)
+    )(order, *blocks, *sums, *pieces)
+
+
+def whole(arrays):
+    return [pl.BlockSpec(array.shape, lambda i: (0, 0)) for array in arrays]
+
+
+def project_last(blocks, sums, pieces, order):
+    count = len(blocks)
+    outs = [sums[0], jax.ShapeDtypeStruct(sums[0].shape, jnp.bfloat16)]
+    return pl.pallas_call(
+        functools.partial(project_kernel, count, count),
+        grid=(1,),
+        in_specs=[pl.BlockSpec(memory_space=pltpu.SMEM)] + whole([*blocks, *sums, *pieces]),
+        out_specs=whole(outs),
+        out_shape=[jax.ShapeDtypeStruct(out.shape, out.dtype) for out in outs],
+        compiler_params=pltpu.CompilerParams(vmem_limit_bytes=20 * 1024 * 1024),
+        name="project_last",
+    )(order, *blocks, *sums, *pieces)
 
 
 def norm_kernel(stream_ref, keep_ref, got_ref, residual_ref, normed_ref):
-    total = stream_ref[...].astype(jnp.float32) + keep_ref[...] + got_ref[...]
+    total = stream_ref[...].astype(jnp.float32) + keep_ref[...] + got_ref[...].astype(jnp.float32)
     residual = total.astype(jnp.bfloat16)
     residual_ref[...] = residual
     widened = residual.astype(jnp.float32)
@@ -233,15 +256,12 @@
 
 
 def add_norm(stream, keep, got):
-    rows, width = stream.shape
     like = jax.ShapeDtypeStruct(stream.shape, jnp.bfloat16)
-    part = rows // 4 if rows % 64 == 0 else rows
-    held = pl.BlockSpec((part, width), lambda i: (i, 0))
     return pl.pallas_call(
         norm_kernel,
-        grid=(rows // part,),
-        in_specs=[held] * 3,
-        out_specs=[held, held],
+        grid=(1,),
+        in_specs=whole([stream, keep, got]),
+        out_specs=whole([like, like]),
         out_shape=[like, like],
         compiler_params=pltpu.CompilerParams(vmem_limit_bytes=20 * 1024 * 1024),
         name="add_norm",
@@ -304,49 +324,40 @@
     mine = jnp.concatenate([keys, jnp.where(live, values, DEAD).astype(values.dtype)], axis=1)
     second = from_behind(mine, "ctx", 4)
     pieces = [out_weight]
-    fourth = crossed = crossed_far = None
+    second, ahead, back, *late = lax.optimization_barrier((second, ahead, back, *own))
+    fourth = from_behind(second, "ctx", 4)
+    crossed = lax.ppermute(jnp.where(side == 0, mine, second), "ctx", flip[1])
+    fourth, crossed = lax.optimization_barrier((fourth, crossed))
+    crossed_far = lax.ppermute(jnp.where(side == 0, second, fourth), "ctx", flip[1])
+    other = [swapped(weight) for weight in late]
+    notes = lax.all_to_all(notes, "ctx", split_axis=0, concat_axis=0, tiled=True)
     for step in range(2, half + 1):
-        if step == 2:
-            second, ahead, back, notes, *late = lax.optimization_barrier(
-                (second, ahead, back, notes, *own)
-            )
-            notes = lax.all_to_all(notes, "ctx", split_axis=0, concat_axis=0, tiled=True)
-            fourth = from_behind(second, "ctx", 4)
-            crossed = lax.ppermute(jnp.where(side == 0, mine, second), "ctx", flip[1])
-            other = [swapped(weight) for weight in late]
-        elif step == 3:
-            fourth, crossed, ahead, back, notes = lax.optimization_barrier(
-                (fourth, crossed, ahead, back, notes)
-            )
-            crossed_far = lax.ppermute(jnp.where(side == 0, second, fourth), "ctx", flip[1])
-        else:
-            ahead, back = lax.optimization_barrier((ahead, back))
         pieces += [far_memory(ahead), far_memory(back)]
-        if step < half:
-            ahead, back = moved(ahead, 1), moved(back, -1)
-    if crossed_far is None:
-        crossed_far = lax.ppermute(jnp.where(side == 0, second, fourth), "ctx", flip[1])
+        if step == half:
+            break
+        ahead, back = moved(ahead, 1), moved(back, -1)
+        ahead, back = lax.optimization_barrier((ahead, back))
     windows = [mine, second, crossed, crossed_far]
     shared = [jnp.where(core == 0, mine, fourth), second, crossed, crossed_far]
     windows += [swapped(window) for window in shared]
-    ahead, notes, *windows = lax.optimization_barrier((ahead, notes, *windows))
-    last = moved(ahead, 1)
-    pieces.append(far_memory(last))
-    attended, kept, given = attend(queries, windows, reached, core)
-    got = swapped(given)
     chosen = (order[:, None] == expert[None])[:, :, None, None]
     picked = jnp.sum(jnp.where(chosen, notes[None], 0.0), axis=1)
     picked = picked.transpose(0, 2, 1).reshape(-1, 2)
 
+    picked, reached = lax.optimization_barrier((picked, reached))
+    attended, kept, given = attend(queries, windows, reached, core)
+    got = swapped(given)
+    ahead, attended = lax.optimization_barrier((ahead, attended))
+    last = moved(ahead, 1)
+    keep, give = project_pieces([kept, got], pieces[:-1], chips)
+    last_two = [pieces[-1], last]
+    keep, give, last_two = lax.optimization_barrier((keep, give, last_two))
     own, other = near_memory(own), near_memory(other)
-    keep, give = project_pieces(kept, got, pieces, chips)
+    keep, give = project_last([kept, got], [keep, give], last_two, chips[-2:])
     residual, normed = add_norm(stream, keep, swapped(give))
 
-    def factors(first, number):
-        return picked[first * rows : (first + number) * rows]
-
     cut = rows // 2
-    (home,) = run_experts([normed], factors(0, 1), own, other)
+    (home,) = run_experts([normed], picked, 0, own, other)
     ahead, back = normed, normed
     done = [home]
     sums = []
@@ -354,12 +365,12 @@
         ahead, back = moved(ahead, 1), moved(back, -1)
         ahead, back, *done = lax.optimization_barrier((ahead, back, *done))
         sums.append(done)
-        done = run_experts([ahead, back], factors(2 * step - 1, 2), own, other)
+        done = run_experts([ahead, back], picked, (2 * step - 1) * rows, own, other)
     far_low, far_high = moved(ahead[:cut], 1), moved(back[cut:], -1)
     far_low, far_high, *done = lax.optimization_barrier((far_low, far_high, *done))
     sums.append(done)
     far_low, far_high = run_experts(
-        [far_low, far_high], factors(2 * half - 1, 1), own, other
+        [far_low, far_high], picked, (2 * half - 1) * rows, own, other
     )
 
     def summed(a, b):

time: 204 us -> 203 us (level)
  waiting for transfers between devices: 80.4 us -> 89 us
  local copies, waits for them, and re-layouts: 12.9 us -> 5.5 us
  Pallas kernels: 58.4 us -> 53.6 us
    ppermute x23, waiting for transfers between devices: 52.7 us -> 64.9 us  [moved(): return lax.ppermute(block, 'ctx', route)]
    unnamed x38 -> x26, local copies, waits for them, and re-layouts: 10.2 us -> 3.68 us
    all_to_all x1, waiting for transfers between devices: 6.08 us -> 0.01 us  [ring_layer(): lax.all_to_all(notes, 'ctx', split_axis=0, concat_axis=0, tiled=True)]
    pallas_call x7 -> x8, Pallas kernels: 46.6 us -> 41.1 us  [the longest x5 34.8 us: run_experts(): pl.pallas_call(functools.partial(expert_kernel, count, first), in_specs=[...]
    ppermute x2, waiting for transfers between devices: 9.68 us -> 12.7 us  [from_behind(): return lax.ppermute(block, axis, route)]
  transfers between devices with their start and end apart: 37 -> 37, of which waited for: 20 -> 21; matrix products, arithmetic and copies ran while one was open for 5% -> 4% of each run, Pallas kernels for 26% -> 24%
where the time goes in v1:
time: 203 us; the launch traced here: 202 us
  waiting for transfers between devices  89 us (44%)
  Pallas kernels  53.6 us (26%)
  starting transfers between devices  43.4 us (21%)
  other arithmetic  8.91 us (4%)
  local copies, waits for them, and re-layouts  5.5 us (3%)
    ppermute x23, waiting for transfers between devices, moved(): return lax.ppermute(block, 'ctx', route)  64.9 us
    pallas_call x5, Pallas kernels, run_experts(): pl.pallas_call(functools.partial(expert_kernel, count, first), in_specs=[...  34.8 us
    ppermute x23, starting transfers between devices, moved(): return lax.ppermute(block, 'ctx', route)  26 us
    ppermute x2, waiting for transfers between devices, from_behind(): return lax.ppermute(block, axis, route)  12.7 us
    pallas_call x1, Pallas kernels, attend(): pl.pallas_call(functools.partial(attend_kernel, pair, len(windows)), grid...  12.5 us
    ppermute x2, starting transfers between devices, from_behind(): return lax.ppermute(block, axis, route)  9.05 us
    ppermute x1, waiting for transfers between devices, ring_layer(): lax.ppermute(jnp.where(side == 0, second, fourth), 'ctx', flip[1])  5.93 us
    ppermute x9, waiting for transfers between devices, swapped(): return lax.ppermute(block, 'ctx', flip[0])  5.34 us
  transfers between devices with their start and end apart: 37, of which 21 were waited for; matrix products, arithmetic and copies ran while one was open for 4% of the time, Pallas kernels for 24%

profile of v1, /device:TPU:0, one launch (start us, length us, event | category | flops | bytes accessed | tf_op | source)
XLA Modules:
  0.0 202.1 jit_solution(2017680630162847856)
XLA Ops:
  0.6 3.1 %collective-permute-start.1 = (bf16[128,2048]{1,0:T(8,128)(2,1)}, bf16[128,2048]{1,0:T(8,128)(2,1)S(1)}, u32[]{:S(2)}, u32[]{:S(2)}) collective-permute-start(bf16[128,2048]{1,0:T(8,128)(2,1)} %refs_2_.2), channel_id=1, source_target_pairs={{0,4},{1,5},{4,8},{5,9},{8,12},{9,13},{12,14},{13,15},{14,10},{15,... | collective-permute-start | bytes 1572872 | tf_op jit(solution)/shard_map/ppermute | solution.py:294
  6.4 3.9 %collective-permute-start = (bf16[256,512]{1,0:T(8,128)(2,1)S(1)}, bf16[256,512]{1,0:T(8,128)(2,1)S(1)}, u32[]{:S(2)}, u32[]{:S(2)}) collective-permute-start(bf16[256,512]{1,0:T(8,128)(2,1)S(1)} %pad_maximum_fusion.2.refs_0_.refs_8_), channel_id=1, source_target_pairs={{0,4},{1,5},{2,6},{3,7},{4,8},{5,9},{6,10},{7,11},{8,12},{9,13},{1... | collective-permute-start | bytes 786440 | tf_op jit(solution)/shard_map/ppermute | solution.py:21
  10.3 10.4 %collective-permute-done.refs_1_.refs_9_ = bf16[256,512]{1,0:T(8,128)(2,1)S(1)} collective-permute-done((bf16[256,512]{1,0:T(8,128)(2,1)S(1)}, bf16[256,512]{1,0:T(8,128)(2,1)S(1)}, u32[]{:S(2)}, u32[]{:S(2)}) %collective-permute-start) | collective-permute-done | bytes 262176 | tf_op jit(solution)/shard_map/ppermute | solution.py:21
  20.8 1.8 broadcast_select_fusion.2
  22.6 1.7 collective-permute-start.8
  24.2 5.1 %collective-permute-start.7 = (bf16[256,512]{1,0:T(8,128)(2,1)S(1)}, bf16[256,512]{1,0:T(8,128)(2,1)}, u32[]{:S(2)}, u32[]{:S(2)}) collective-permute-start(bf16[256,512]{1,0:T(8,128)(2,1)S(1)} %collective-permute-done.refs_1_.refs_9_), channel_id=1, source_target_pairs={{0,4},{1,5},{2,6},{3,7},{4,8},{5,9},{6,10},{7,11},{8,12},{9,13},{1... | collective-permute-start | bytes 786440 | tf_op jit(solution)/shard_map/ppermute | solution.py:21
  30.5 2.3 %collective-permute-done.7 = bf16[256,512]{1,0:T(8,128)(2,1)} collective-permute-done((bf16[256,512]{1,0:T(8,128)(2,1)S(1)}, bf16[256,512]{1,0:T(8,128)(2,1)}, u32[]{:S(2)}, u32[]{:S(2)}) %collective-permute-start.7) | collective-permute-done | bytes 262176 | tf_op jit(solution)/shard_map/ppermute | solution.py:21
  32.8 1.1 broadcast_select_fusion
  34.6 5.9 %collective-permute-done.9.refs_3_.refs_11_ = bf16[256,512]{1,0:T(8,128)(2,1)} collective-permute-done((bf16[256,512]{1,0:T(8,128)(2,1)S(1)}, bf16[256,512]{1,0:T(8,128)(2,1)}, u32[]{:S(2)}, u32[]{:S(2)}) %collective-permute-start.9) | collective-permute-done | bytes 262176 | tf_op jit(solution)/shard_map/ppermute | solution.py:331
  40.5 2.5 %collective-permute-start.3 = (bf16[128,2048]{1,0:T(8,128)(2,1)}, bf16[128,2048]{1,0:T(8,128)(2,1)}, u32[]{:S(2)}, u32[]{:S(2)}) collective-permute-start(bf16[128,2048]{1,0:T(8,128)(2,1)} %copy-done.11), channel_id=1, source_target_pairs={{0,4},{1,5},{4,8},{5,9},{8,12},{9,13},{12,14},{13,15},{14,10},{15,... | collective-permute-start | bytes 1572872 | tf_op jit(solution)/shard_map/ppermute | solution.py:294
  43.0 1.8 collective-permute-done.10.refs_4_.refs_12_
  47.2 4.5 %all-to-all-start = ((f32[16,2,128]{2,1,0:T(2,128)}), f32[16,2,128]{2,1,0:T(2,128)S(1)}, u32[]{:S(2)}, u32[]{:S(2)}) async-start(f32[16,2,128]{2,1,0:T(2,128)} %copy.17), calls=%async_computation | async-start | bytes 32768 | tf_op jit(solution)/shard_map/all_to_all | solution.py:333
  52.2 7.9 %collective-permute-done.4.refs_6_ = bf16[128,2048]{1,0:T(8,128)(2,1)} collective-permute-done((bf16[128,2048]{1,0:T(8,128)(2,1)}, bf16[128,2048]{1,0:T(8,128)(2,1)}, u32[]{:S(2)}, u32[]{:S(2)}) %collective-permute-start.4) | collective-permute-done | bytes 524320 | tf_op jit(solution)/shard_map/ppermute | solution.py:294
  63.7 1.0 copy.19
  65.7 1.0 copy-done.8
  67.7 12.5 %attend.1 = (bf16[128,2048]{1,0:T(8,128)(2,1)}, bf16[128,1024]{1,0:T(8,128)(2,1)S(1)}, bf16[128,1024]{1,0:T(8,128)(2,1)S(1)}) custom-call(s32[8]{0:T(128)S(1)} %compare_convert_fusion.length_ref, s32[1]{0:T(128)} %bitcast.8.core_ref, bf16[128,2048]{1,0:T(8,128)(2,1)S(1)} %copy-done.8, bf16[256,512]{1,0:T(8,128)(2,1)S(1)} %copy-done.7, ...), custom_call_target="tpu_custom_call" | custom-call | flops 2147483648 | bytes 3145728 | tf_op jit(solution)/shard_map/attend/pallas_call | solution.py:98
  80.2 1.2 collective-permute-start.15
  81.4 1.5 collective-permute-done.14.refs_1_
  82.9 4.4 %project.1 = (f32[128,2048]{1,0:T(8,128)S(1)}, f32[128,2048]{1,0:T(8,128)S(1)}) custom-call(s32[8]{0:T(128)S(1)} %get-tuple-element.107.order_ref, bf16[128,1024]{1,0:T(8,128)(2,1)S(1)} %get-tuple-element.65.refs_0_, bf16[128,1024]{1,0:T(8,128)(2,1)S(1)} %collective-permute-done.14.refs_1_, bf16[128,2048]{1,0:T(8,128)(2,1)S(1)} %copy-done.4, ...), custom_call_target="tpu_custom_call" | custom-call | flops 805306368 | bytes 5242880 | tf_op jit(solution)/shard_map/project/pallas_call | solution.py:210
  87.3 6.9 %collective-permute-done.15.refs_5_ = bf16[128,2048]{1,0:T(8,128)(2,1)S(1)} collective-permute-done((bf16[128,2048]{1,0:T(8,128)(2,1)}, bf16[128,2048]{1,0:T(8,128)(2,1)S(1)}, u32[]{:S(2)}, u32[]{:S(2)}) %collective-permute-start.15) | collective-permute-done | bytes 524320 | tf_op jit(solution)/shard_map/ppermute | solution.py:294
  94.2 1.5 project_last.1
  95.8 1.9 collective-permute-done.16.got_ref
  98.0 1.1 collective-permute-start.17
  100.2 5.6 %experts.5 = bf16[128,2048]{1,0:T(8,128)(2,1)S(1)} custom-call(bf16[128,2048]{1,0:T(8,128)(2,1)S(1)} %get-tuple-element.78.refs_0_, f32[1024,2]{1,0:T(8,128)S(1)} %bitcast.10, bf16[1,2048,768]{2,1,0:T(8,128)(2,1)S(1)} %copy-done, bf16[1,2048,768]{2,1,0:T(8,128)(2,1)S(1)} %copy-done.1, bf16[1,768,2048]{2,1,0:T(8,128)(2,1)S(1)} %copy-done.2, ...), custom_call_target="tpu_custom_call" | custom-call | flops 2415919104 | bytes 19922944 | tf_op jit(solution)/shard_map/experts/pallas_call | solution.py:154
  105.7 6.3 %collective-permute-done.17.refs_0_ = bf16[128,2048]{1,0:T(8,128)(2,1)S(1)} collective-permute-done((bf16[128,2048]{1,0:T(8,128)(2,1)S(1)}, bf16[128,2048]{1,0:T(8,128)(2,1)S(1)}, u32[]{:S(2)}, u32[]{:S(2)}) %collective-permute-start.17) | collective-permute-done | bytes 524320 | tf_op jit(solution)/shard_map/ppermute | solution.py:294
  112.8 1.5 collective-permute-start.22
  114.8 7.9 %experts.6 = (bf16[128,2048]{1,0:T(8,128)(2,1)S(1)}, bf16[128,2048]{1,0:T(8,128)(2,1)S(1)}) custom-call(bf16[128,2048]{1,0:T(8,128)(2,1)S(1)} %collective-permute-done.17.refs_0_, bf16[128,2048]{1,0:T(8,128)(2,1)S(1)} %collective-permute-done.18.refs_1_, f32[1024,2]{1,0:T(8,128)S(1)} %bitcast.11, bf16[1,2048,768]{2,1,0:T(8,128)(2,1)S(1)} %copy-done, ...), custom_call_target="tpu_custom_call" | custom-call | flops 4831838208 | bytes 20971520 | tf_op jit(solution)/shard_map/experts/pallas_call | solution.py:154
  122.8 2.9 %collective-permute-done.22.refs_0_ = bf16[128,2048]{1,0:T(8,128)(2,1)S(1)} collective-permute-done((bf16[128,2048]{1,0:T(8,128)(2,1)S(1)}, bf16[128,2048]{1,0:T(8,128)(2,1)S(1)}, u32[]{:S(2)}, u32[]{:S(2)}) %collective-permute-start.22) | collective-permute-done | bytes 524320 | tf_op jit(solution)/shard_map/ppermute | solution.py:294
  125.6 1.2 collective-permute-done.23.refs_1_
  128.9 7.9 %experts.7 = (bf16[128,2048]{1,0:T(8,128)(2,1)S(1)}, bf16[128,2048]{1,0:T(8,128)(2,1)S(1)}) custom-call(bf16[128,2048]{1,0:T(8,128)(2,1)S(1)} %collective-permute-done.22.refs_0_, bf16[128,2048]{1,0:T(8,128)(2,1)S(1)} %collective-permute-done.23.refs_1_, f32[1024,2]{1,0:T(8,128)S(1)} %bitcast.12, bf16[1,2048,768]{2,1,0:T(8,128)(2,1)S(1)} %copy-done, ...), custom_call_target="tpu_custom_call" | custom-call | flops 4831838208 | bytes 20971520 | tf_op jit(solution)/shard_map/experts/pallas_call | solution.py:154
  136.8 1.8 collective-permute-done.24.refs_0_
  140.2 1.5 collective-permute-start.27
  141.7 7.9 %experts.8 = (bf16[128,2048]{1,0:T(8,128)(2,1)S(1)}, bf16[128,2048]{1,0:T(8,128)(2,1)S(1)}) custom-call(bf16[128,2048]{1,0:T(8,128)(2,1)S(1)} %collective-permute-done.24.refs_0_, bf16[128,2048]{1,0:T(8,128)(2,1)S(1)} %collective-permute-done.25.refs_1_, f32[1024,2]{1,0:T(8,128)S(1)} %bitcast.13, bf16[1,2048,768]{2,1,0:T(8,128)(2,1)S(1)} %copy-done, ...), custom_call_target="tpu_custom_call" | custom-call | flops 4831838208 | bytes 20971520 | tf_op jit(solution)/shard_map/experts/pallas_call | solution.py:154
  149.7 5.6 %experts.9 = (bf16[64,2048]{1,0:T(8,128)(2,1)S(1)}, bf16[64,2048]{1,0:T(8,128)(2,1)S(1)}) custom-call(bf16[64,2048]{1,0:T(8,128)(2,1)S(1)} %collective-permute-done.26.refs_0_, bf16[64,2048]{1,0:T(8,128)(2,1)S(1)} %collective-permute-done.27.refs_1_, f32[1024,2]{1,0:T(8,128)S(1)} %bitcast.14, bf16[1,2048,768]{2,1,0:T(8,128)(2,1)S(1)} %copy-done, ...), custom_call_target="tpu_custom_call" | custom-call | flops 2415919104 | bytes 19922944 | tf_op jit(solution)/shard_map/experts/pallas_call | solution.py:154
  155.2 1.0 collective-permute-start.28
  156.3 1.1 collective-permute-start.32
  157.4 6.5 %collective-permute-done.28 = bf16[64,2048]{1,0:T(8,128)(2,1)S(1)} collective-permute-done((bf16[64,2048]{1,0:T(8,128)(2,1)S(1)}, bf16[64,2048]{1,0:T(8,128)(2,1)S(1)}, u32[]{:S(2)}, u32[]{:S(2)}) %collective-permute-start.28) | collective-permute-done | bytes 262176 | tf_op jit(solution)/shard_map/ppermute | solution.py:294
  164.0 1.0 collective-permute-start.29
  165.2 1.1 collective-permute-start.33
  166.3 10.2 %collective-permute-done.29 = bf16[128,2048]{1,0:T(8,128)(2,1)S(1)} collective-permute-done((bf16[128,2048]{1,0:T(8,128)(2,1)S(1)}, bf16[128,2048]{1,0:T(8,128)(2,1)S(1)}, u32[]{:S(2)}, u32[]{:S(2)}) %collective-permute-start.29) | collective-permute-done | bytes 524320 | tf_op jit(solution)/shard_map/ppermute | solution.py:294
  176.7 1.0 collective-permute-start.30
  177.9 1.1 collective-permute-start.34
  179.0 11.5 %collective-permute-done.30 = bf16[128,2048]{1,0:T(8,128)(2,1)S(1)} collective-permute-done((bf16[128,2048]{1,0:T(8,128)(2,1)S(1)}, bf16[128,2048]{1,0:T(8,128)(2,1)S(1)}, u32[]{:S(2)}, u32[]{:S(2)}) %collective-permute-start.30) | collective-permute-done | bytes 524320 | tf_op jit(solution)/shard_map/ppermute | solution.py:294
  190.6 1.0 collective-permute-start.31
  191.7 1.1 collective-permute-start.35
  192.8 7.0 %collective-permute-done.31 = bf16[128,2048]{1,0:T(8,128)(2,1)S(1)} collective-permute-done((bf16[128,2048]{1,0:T(8,128)(2,1)S(1)}, bf16[128,2048]{1,0:T(8,128)(2,1)S(1)}, u32[]{:S(2)}, u32[]{:S(2)}) %collective-permute-start.31) | collective-permute-done | bytes 524320 | tf_op jit(solution)/shard_map/ppermute | solution.py:294
  199.8 1.2 collective-permute-done.35
  201.0 1.1 add_convert_fusion
  (90 shorter events, 19.3 us)
Async XLA Ops:
  0.6 20.1 %collective-permute-start.1 = (bf16[128,2048]{1,0:T(8,128)(2,1)}, bf16[128,2048]{1,0:T(8,128)(2,1)S(1)}, u32[]{:S(2)}, u32[]{:S(2)}) collective-permute-start(bf16[128,2048]{1,0:T(8,128)(2,1)} %refs_2_.2), channel_id=1, source_target_pairs={{0,4},{1,5},{4,8},{5,9},{8,12},{9,13},{12,14},{13,15},{14,10},{15,... | collective-permute-start | bytes 1572872 | tf_op jit(solution)/shard_map/ppermute | solution.py:294
  3.7 17.0 %collective-permute-start.2 = (bf16[128,2048]{1,0:T(8,128)(2,1)}, bf16[128,2048]{1,0:T(8,128)(2,1)S(1)}, u32[]{:S(2)}, u32[]{:S(2)}) collective-permute-start(bf16[128,2048]{1,0:T(8,128)(2,1)} %refs_2_.2), channel_id=1, source_target_pairs={{0,2},{1,3},{4,0},{5,1},{8,4},{9,5},{12,8},{13,9},{14,12},{15,13},... | collective-permute-start | bytes 1572872 | tf_op jit(solution)/shard_map/ppermute | solution.py:294
  6.4 23.0 %copy-start.6 = (bf16[256,512]{1,0:T(8,128)(2,1)}, bf16[256,512]{1,0:T(8,128)(2,1)S(1)}, u32[]{:S(2)}) copy-start(bf16[256,512]{1,0:T(8,128)(2,1)S(1)} %pad_maximum_fusion.2.refs_0_.refs_8_) | copy-start | bytes 786436
  6.4 14.4 %collective-permute-start = (bf16[256,512]{1,0:T(8,128)(2,1)S(1)}, bf16[256,512]{1,0:T(8,128)(2,1)S(1)}, u32[]{:S(2)}, u32[]{:S(2)}) collective-permute-start(bf16[256,512]{1,0:T(8,128)(2,1)S(1)} %pad_maximum_fusion.2.refs_0_.refs_8_), channel_id=1, source_target_pairs={{0,4},{1,5},{2,6},{3,7},{4,8},{5,9},{6,10},{7,11},{8,12},{9,13},{1... | collective-permute-start | bytes 786440 | tf_op jit(solution)/shard_map/ppermute | solution.py:21
  20.7 8.6 %copy-start.11 = (bf16[128,2048]{1,0:T(8,128)(2,1)}, bf16[128,2048]{1,0:T(8,128)(2,1)S(1)}, u32[]{:S(2)}) copy-start(bf16[128,2048]{1,0:T(8,128)(2,1)S(1)} %collective-permute-done.1.refs_3_) | copy-start | bytes 1572868
  20.8 8.6 %copy-start.12 = (bf16[128,2048]{1,0:T(8,128)(2,1)}, bf16[128,2048]{1,0:T(8,128)(2,1)S(1)}, u32[]{:S(2)}) copy-start(bf16[128,2048]{1,0:T(8,128)(2,1)S(1)} %collective-permute-done.2.refs_4_) | copy-start | bytes 1572868
  22.6 7.5 %collective-permute-start.8 = (bf16[256,512]{1,0:T(8,128)(2,1)}, bf16[256,512]{1,0:T(8,128)(2,1)}, u32[]{:S(2)}, u32[]{:S(2)}) collective-permute-start(bf16[256,512]{1,0:T(8,128)(2,1)} %broadcast_select_fusion.2), channel_id=1, source_target_pairs={{0,2},{1,3},{2,0},{3,1},{4,6},{5,7},{6,4},{7,5},{8,10},{9,11},{10,... | collective-permute-start | bytes 786440 | tf_op jit(solution)/shard_map/ppermute | solution.py:329
  24.2 8.5 %collective-permute-start.7 = (bf16[256,512]{1,0:T(8,128)(2,1)S(1)}, bf16[256,512]{1,0:T(8,128)(2,1)}, u32[]{:S(2)}, u32[]{:S(2)}) collective-permute-start(bf16[256,512]{1,0:T(8,128)(2,1)S(1)} %collective-permute-done.refs_1_.refs_9_), channel_id=1, source_target_pairs={{0,4},{1,5},{2,6},{3,7},{4,8},{5,9},{6,10},{7,11},{8,12},{9,13},{1... | collective-permute-start | bytes 786440 | tf_op jit(solution)/shard_map/ppermute | solution.py:21
  29.4 5.2 %collective-permute-start.11 = (bf16[256,512]{1,0:T(8,128)(2,1)S(1)}, bf16[256,512]{1,0:T(8,128)(2,1)}, u32[]{:S(2)}, u32[]{:S(2)}) collective-permute-start(bf16[256,512]{1,0:T(8,128)(2,1)S(1)} %collective-permute-done.refs_1_.refs_9_), channel_id=1, source_target_pairs={{0,1},{1,0},{2,3},{3,2},{4,5},{5,4},{6,7},{7,6},{8,9},{9,8},{10,11... | collective-permute-start | bytes 786440 | tf_op jit(solution)/shard_map/ppermute | solution.py:297
  29.4 70.7 %collective-permute-start.19 = (bf16[1,2048,768]{2,1,0:T(8,128)(2,1)}, bf16[1,2048,768]{2,1,0:T(8,128)(2,1)S(1)}, u32[]{:S(2)}, u32[]{:S(2)}) collective-permute-start(bf16[1,2048,768]{2,1,0:T(8,128)(2,1)} %refs_3_.9), channel_id=1, source_target_pairs={{0,1},{1,0},{2,3},{3,2},{4,5},{5,4},{6,7},{7,6},{8,9},{9,8},{10,11... | collective-permute-start | bytes 9437192 | tf_op jit(solution)/shard_map/ppermute | solution.py:297
  29.9 70.2 %collective-permute-start.20 = (bf16[1,2048,768]{2,1,0:T(8,128)(2,1)}, bf16[1,2048,768]{2,1,0:T(8,128)(2,1)}, u32[]{:S(2)}, u32[]{:S(2)}) collective-permute-start(bf16[1,2048,768]{2,1,0:T(8,128)(2,1)} %refs_4_.9), channel_id=1, source_target_pairs={{0,1},{1,0},{2,3},{3,2},{4,5},{5,4},{6,7},{7,6},{8,9},{9,8},{10,11... | collective-permute-start | bytes 9437192 | tf_op jit(solution)/shard_map/ppermute | solution.py:297
  30.1 70.1 %collective-permute-start.21 = (bf16[1,768,2048]{2,1,0:T(8,128)(2,1)}, bf16[1,768,2048]{2,1,0:T(8,128)(2,1)}, u32[]{:S(2)}, u32[]{:S(2)}) collective-permute-start(bf16[1,768,2048]{2,1,0:T(8,128)(2,1)} %refs_5_.7), channel_id=1, source_target_pairs={{0,1},{1,0},{2,3},{3,2},{4,5},{5,4},{6,7},{7,6},{8,9},{9,8},{10,11... | collective-permute-start | bytes 9437192 | tf_op jit(solution)/shard_map/ppermute | solution.py:297
  33.9 6.6 %collective-permute-start.9 = (bf16[256,512]{1,0:T(8,128)(2,1)S(1)}, bf16[256,512]{1,0:T(8,128)(2,1)}, u32[]{:S(2)}, u32[]{:S(2)}) collective-permute-start(bf16[256,512]{1,0:T(8,128)(2,1)S(1)} %get-tuple-element.109), channel_id=1, source_target_pairs={{0,2},{1,3},{2,0},{3,1},{4,6},{5,7},{6,4},{7,5},{8,10},{9,11},{10,... | collective-permute-start | bytes 786440 | tf_op jit(solution)/shard_map/ppermute | solution.py:331
  34.6 10.2 %collective-permute-start.10 = (bf16[256,512]{1,0:T(8,128)(2,1)S(1)}, bf16[256,512]{1,0:T(8,128)(2,1)S(1)}, u32[]{:S(2)}, u32[]{:S(2)}) collective-permute-start(bf16[256,512]{1,0:T(8,128)(2,1)S(1)} %get-tuple-element.108), channel_id=1, source_target_pairs={{0,1},{1,0},{2,3},{3,2},{4,5},{5,4},{6,7},{7,6},{8,9},{9,8},{10,11... | collective-permute-start | bytes 786440 | tf_op jit(solution)/shard_map/ppermute | solution.py:297
  40.5 11.2 %collective-permute-start.3 = (bf16[128,2048]{1,0:T(8,128)(2,1)}, bf16[128,2048]{1,0:T(8,128)(2,1)}, u32[]{:S(2)}, u32[]{:S(2)}) collective-permute-start(bf16[128,2048]{1,0:T(8,128)(2,1)} %copy-done.11), channel_id=1, source_target_pairs={{0,4},{1,5},{4,8},{5,9},{8,12},{9,13},{12,14},{13,15},{14,10},{15,... | collective-permute-start | bytes 1572872 | tf_op jit(solution)/shard_map/ppermute | solution.py:294
  45.5 14.6 %collective-permute-start.4 = (bf16[128,2048]{1,0:T(8,128)(2,1)}, bf16[128,2048]{1,0:T(8,128)(2,1)}, u32[]{:S(2)}, u32[]{:S(2)}) collective-permute-start(bf16[128,2048]{1,0:T(8,128)(2,1)} %copy-done.12), channel_id=1, source_target_pairs={{0,2},{1,3},{4,0},{5,1},{8,4},{9,5},{12,8},{13,9},{14,12},{15,13},... | collective-permute-start | bytes 1572872 | tf_op jit(solution)/shard_map/ppermute | solution.py:294
  47.2 16.3 %all-to-all-start = ((f32[16,2,128]{2,1,0:T(2,128)}), f32[16,2,128]{2,1,0:T(2,128)S(1)}, u32[]{:S(2)}, u32[]{:S(2)}) async-start(f32[16,2,128]{2,1,0:T(2,128)} %copy.17), calls=%async_computation | async-start | bytes 32768 | tf_op jit(solution)/shard_map/all_to_all | solution.py:333
  51.7 9.1 %collective-permute-start.12 = (bf16[256,512]{1,0:T(8,128)(2,1)}, bf16[256,512]{1,0:T(8,128)(2,1)}, u32[]{:S(2)}, u32[]{:S(2)}) collective-permute-start(bf16[256,512]{1,0:T(8,128)(2,1)} %collective-permute-done.8.refs_2_.refs_10_), channel_id=1, source_target_pairs={{0,1},{1,0},{2,3},{3,2},{4,5},{5,4},{6,7},{7,6},{8,9},{9,8},{10,11... | collective-permute-start | bytes 786440 | tf_op jit(solution)/shard_map/ppermute | solution.py:297
  60.1 1.9 collective-permute-start.13
  60.9 19.3 %collective-permute-start.5 = (bf16[128,2048]{1,0:T(8,128)(2,1)}, bf16[128,2048]{1,0:T(8,128)(2,1)}, u32[]{:S(2)}, u32[]{:S(2)}) collective-permute-start(bf16[128,2048]{1,0:T(8,128)(2,1)} %collective-permute-done.3.refs_5_), channel_id=1, source_target_pairs={{0,4},{1,5},{4,8},{5,9},{8,12},{9,13},{12,14},{13,15},{14,10},{15,... | collective-permute-start | bytes 1572872 | tf_op jit(solution)/shard_map/ppermute | solution.py:294
  62.0 18.1 %collective-permute-start.6 = (bf16[128,2048]{1,0:T(8,128)(2,1)}, bf16[128,2048]{1,0:T(8,128)(2,1)}, u32[]{:S(2)}, u32[]{:S(2)}) collective-permute-start(bf16[128,2048]{1,0:T(8,128)(2,1)} %collective-permute-done.4.refs_6_), channel_id=1, source_target_pairs={{0,2},{1,3},{4,0},{5,1},{8,4},{9,5},{12,8},{13,9},{14,12},{15,13},... | collective-permute-start | bytes 1572872 | tf_op jit(solution)/shard_map/ppermute | solution.py:294
  64.7 0.9 copy-start.7
  65.7 1.0 copy-start.8
  67.7 15.2 %copy-start.4 = (bf16[128,2048]{1,0:T(8,128)(2,1)S(1)}, bf16[128,2048]{1,0:T(8,128)(2,1)}, u32[]{:S(2)}) copy-start(bf16[128,2048]{1,0:T(8,128)(2,1)} %refs_2_.2) | copy-start | bytes 1572868
  67.7 30.0 %copy-start.5 = (bf16[128,2048]{1,0:T(8,128)(2,1)S(1)}, bf16[128,2048]{1,0:T(8,128)(2,1)}, u32[]{:S(2)}) copy-start(bf16[128,2048]{1,0:T(8,128)(2,1)} %stream_ref.1) | copy-start | bytes 1572868
  67.7 32.5 %copy-start.3 = (f32[8,128,2]{2,1,0:T(8,128)S(1)}, f32[8,128,2]{2,1,0:T(8,128)}, u32[]{:S(2)}) copy-start(f32[8,128,2]{2,1,0:T(8,128)} %copy.19) | copy-start | bytes 24580
  80.2 14.0 %collective-permute-start.15 = (bf16[128,2048]{1,0:T(8,128)(2,1)}, bf16[128,2048]{1,0:T(8,128)(2,1)S(1)}, u32[]{:S(2)}, u32[]{:S(2)}) collective-permute-start(bf16[128,2048]{1,0:T(8,128)(2,1)} %collective-permute-done.5.refs_7_), channel_id=1, source_target_pairs={{0,4},{1,5},{4,8},{5,9},{8,12},{9,13},{12,14},{13,15},{14,10},{15,... | collective-permute-start | bytes 1572872 | tf_op jit(solution)/shard_map/ppermute | solution.py:294
  81.3 1.5 collective-permute-start.14
  82.9 17.3 %copy-start.1 = (bf16[1,2048,768]{2,1,0:T(8,128)(2,1)S(1)}, bf16[1,2048,768]{2,1,0:T(8,128)(2,1)}, u32[]{:S(2)}) copy-start(bf16[1,2048,768]{2,1,0:T(8,128)(2,1)} %refs_4_.9) | copy-start | bytes 9437188
  82.9 17.3 %copy-start.2 = (bf16[1,768,2048]{2,1,0:T(8,128)(2,1)S(1)}, bf16[1,768,2048]{2,1,0:T(8,128)(2,1)}, u32[]{:S(2)}) copy-start(bf16[1,768,2048]{2,1,0:T(8,128)(2,1)} %refs_5_.7) | copy-start | bytes 9437188
  87.3 12.8 %copy-start = (bf16[1,2048,768]{2,1,0:T(8,128)(2,1)S(1)}, bf16[1,2048,768]{2,1,0:T(8,128)(2,1)}, u32[]{:S(2)}) copy-start(bf16[1,2048,768]{2,1,0:T(8,128)(2,1)} %refs_3_.9) | copy-start | bytes 9437188
  95.7 2.0 collective-permute-start.16
  98.0 14.0 %collective-permute-start.17 = (bf16[128,2048]{1,0:T(8,128)(2,1)S(1)}, bf16[128,2048]{1,0:T(8,128)(2,1)S(1)}, u32[]{:S(2)}, u32[]{:S(2)}) collective-permute-start(bf16[128,2048]{1,0:T(8,128)(2,1)S(1)} %get-tuple-element.78.refs_0_), channel_id=1, source_target_pairs={{0,4},{1,5},{4,8},{5,9},{8,12},{9,13},{12,14},{13,15},{14,10},{15,... | collective-permute-start | bytes 1572872 | tf_op jit(solution)/shard_map/ppermute | solution.py:294
  99.1 13.7 %collective-permute-start.18 = (bf16[128,2048]{1,0:T(8,128)(2,1)S(1)}, bf16[128,2048]{1,0:T(8,128)(2,1)S(1)}, u32[]{:S(2)}, u32[]{:S(2)}) collective-permute-start(bf16[128,2048]{1,0:T(8,128)(2,1)S(1)} %get-tuple-element.78.refs_0_), channel_id=1, source_target_pairs={{0,2},{1,3},{4,0},{5,1},{8,4},{9,5},{12,8},{13,9},{14,12},{15,13},... | collective-permute-start | bytes 1572872 | tf_op jit(solution)/shard_map/ppermute | solution.py:294
  112.8 12.8 %collective-permute-start.22 = (bf16[128,2048]{1,0:T(8,128)(2,1)S(1)}, bf16[128,2048]{1,0:T(8,128)(2,1)S(1)}, u32[]{:S(2)}, u32[]{:S(2)}) collective-permute-start(bf16[128,2048]{1,0:T(8,128)(2,1)S(1)} %collective-permute-done.17.refs_0_), channel_id=1, source_target_pairs={{0,4},{1,5},{4,8},{5,9},{8,12},{9,13},{12,14},{13,15},{14,10},{15,... | collective-permute-start | bytes 1572872 | tf_op jit(solution)/shard_map/ppermute | solution.py:294
  114.3 12.5 %collective-permute-start.23 = (bf16[128,2048]{1,0:T(8,128)(2,1)S(1)}, bf16[128,2048]{1,0:T(8,128)(2,1)S(1)}, u32[]{:S(2)}, u32[]{:S(2)}) collective-permute-start(bf16[128,2048]{1,0:T(8,128)(2,1)S(1)} %collective-permute-done.18.refs_1_), channel_id=1, source_target_pairs={{0,2},{1,3},{4,0},{5,1},{8,4},{9,5},{12,8},{13,9},{14,12},{15,13},... | collective-permute-start | bytes 1572872 | tf_op jit(solution)/shard_map/ppermute | solution.py:294
  126.9 11.7 %collective-permute-start.24 = (bf16[128,2048]{1,0:T(8,128)(2,1)S(1)}, bf16[128,2048]{1,0:T(8,128)(2,1)S(1)}, u32[]{:S(2)}, u32[]{:S(2)}) collective-permute-start(bf16[128,2048]{1,0:T(8,128)(2,1)S(1)} %collective-permute-done.22.refs_0_), channel_id=1, source_target_pairs={{0,4},{1,5},{4,8},{5,9},{8,12},{9,13},{12,14},{13,15},{14,10},{15,... | collective-permute-start | bytes 1572872 | tf_op jit(solution)/shard_map/ppermute | solution.py:294
  127.9 11.4 %collective-permute-start.25 = (bf16[128,2048]{1,0:T(8,128)(2,1)S(1)}, bf16[128,2048]{1,0:T(8,128)(2,1)S(1)}, u32[]{:S(2)}, u32[]{:S(2)}) collective-permute-start(bf16[128,2048]{1,0:T(8,128)(2,1)S(1)} %collective-permute-done.23.refs_1_), channel_id=1, source_target_pairs={{0,2},{1,3},{4,0},{5,1},{8,4},{9,5},{12,8},{13,9},{14,12},{15,13},... | collective-permute-start | bytes 1572872 | tf_op jit(solution)/shard_map/ppermute | solution.py:294
  139.3 10.3 %collective-permute-start.26 = (bf16[64,2048]{1,0:T(8,128)(2,1)S(1)}, bf16[64,2048]{1,0:T(8,128)(2,1)S(1)}, u32[]{:S(2)}, u32[]{:S(2)}) collective-permute-start(bf16[64,2048]{1,0:T(8,128)(2,1)S(1)} %slice.22), channel_id=1, source_target_pairs={{0,4},{1,5},{4,8},{5,9},{8,12},{9,13},{12,14},{13,15},{14,10},{15,... | collective-permute-start | bytes 786440 | tf_op jit(solution)/shard_map/ppermute | solution.py:294
  140.2 9.4 %collective-permute-start.27 = (bf16[64,2048]{1,0:T(8,128)(2,1)S(1)}, bf16[64,2048]{1,0:T(8,128)(2,1)S(1)}, u32[]{:S(2)}, u32[]{:S(2)}) collective-permute-start(bf16[64,2048]{1,0:T(8,128)(2,1)S(1)} %slice.23), channel_id=1, source_target_pairs={{0,2},{1,3},{4,0},{5,1},{8,4},{9,5},{12,8},{13,9},{14,12},{15,13},... | collective-permute-start | bytes 786440 | tf_op jit(solution)/shard_map/ppermute | solution.py:294
  155.2 8.6 %collective-permute-start.28 = (bf16[64,2048]{1,0:T(8,128)(2,1)S(1)}, bf16[64,2048]{1,0:T(8,128)(2,1)S(1)}, u32[]{:S(2)}, u32[]{:S(2)}) collective-permute-start(bf16[64,2048]{1,0:T(8,128)(2,1)S(1)} %get-tuple-element.98), channel_id=1, source_target_pairs={{0,2},{1,3},{4,0},{5,1},{8,4},{9,5},{12,8},{13,9},{14,12},{15,13},... | collective-permute-start | bytes 786440 | tf_op jit(solution)/shard_map/ppermute | solution.py:294
  156.3 8.8 %collective-permute-start.32 = (bf16[64,2048]{1,0:T(8,128)(2,1)S(1)}, bf16[64,2048]{1,0:T(8,128)(2,1)S(1)}, u32[]{:S(2)}, u32[]{:S(2)}) collective-permute-start(bf16[64,2048]{1,0:T(8,128)(2,1)S(1)} %get-tuple-element.103), channel_id=1, source_target_pairs={{0,4},{1,5},{4,8},{5,9},{8,12},{9,13},{12,14},{13,15},{14,10},{15,... | collective-permute-start | bytes 786440 | tf_op jit(solution)/shard_map/ppermute | solution.py:294
  164.0 12.6 %collective-permute-start.29 = (bf16[128,2048]{1,0:T(8,128)(2,1)S(1)}, bf16[128,2048]{1,0:T(8,128)(2,1)S(1)}, u32[]{:S(2)}, u32[]{:S(2)}) collective-permute-start(bf16[128,2048]{1,0:T(8,128)(2,1)S(1)} %pad_maximum_fusion), channel_id=1, source_target_pairs={{0,2},{1,3},{4,0},{5,1},{8,4},{9,5},{12,8},{13,9},{14,12},{15,13},... | collective-permute-start | bytes 1572872 | tf_op jit(solution)/shard_map/ppermute | solution.py:294
  165.2 12.5 %collective-permute-start.33 = (bf16[128,2048]{1,0:T(8,128)(2,1)S(1)}, bf16[128,2048]{1,0:T(8,128)(2,1)S(1)}, u32[]{:S(2)}, u32[]{:S(2)}) collective-permute-start(bf16[128,2048]{1,0:T(8,128)(2,1)S(1)} %pad_maximum_fusion.1), channel_id=1, source_target_pairs={{0,4},{1,5},{4,8},{5,9},{8,12},{9,13},{12,14},{13,15},{14,10},{15,... | collective-permute-start | bytes 1572872 | tf_op jit(solution)/shard_map/ppermute | solution.py:294
  176.7 13.7 %collective-permute-start.30 = (bf16[128,2048]{1,0:T(8,128)(2,1)S(1)}, bf16[128,2048]{1,0:T(8,128)(2,1)S(1)}, u32[]{:S(2)}, u32[]{:S(2)}) collective-permute-start(bf16[128,2048]{1,0:T(8,128)(2,1)S(1)} %add_convert_fusion.4), channel_id=1, source_target_pairs={{0,2},{1,3},{4,0},{5,1},{8,4},{9,5},{12,8},{13,9},{14,12},{15,13},... | collective-permute-start | bytes 1572872 | tf_op jit(solution)/shard_map/ppermute | solution.py:294
  177.9 13.7 %collective-permute-start.34 = (bf16[128,2048]{1,0:T(8,128)(2,1)S(1)}, bf16[128,2048]{1,0:T(8,128)(2,1)S(1)}, u32[]{:S(2)}, u32[]{:S(2)}) collective-permute-start(bf16[128,2048]{1,0:T(8,128)(2,1)S(1)} %add_convert_fusion.2), channel_id=1, source_target_pairs={{0,4},{1,5},{4,8},{5,9},{8,12},{9,13},{12,14},{13,15},{14,10},{15,... | collective-permute-start | bytes 1572872 | tf_op jit(solution)/shard_map/ppermute | solution.py:294
  190.6 9.2 %collective-permute-start.31 = (bf16[128,2048]{1,0:T(8,128)(2,1)S(1)}, bf16[128,2048]{1,0:T(8,128)(2,1)S(1)}, u32[]{:S(2)}, u32[]{:S(2)}) collective-permute-start(bf16[128,2048]{1,0:T(8,128)(2,1)S(1)} %add_convert_fusion.3), channel_id=1, source_target_pairs={{0,2},{1,3},{4,0},{5,1},{8,4},{9,5},{12,8},{13,9},{14,12},{15,13},... | collective-permute-start | bytes 1572872 | tf_op jit(solution)/shard_map/ppermute | solution.py:294
  191.7 9.2 %collective-permute-start.35 = (bf16[128,2048]{1,0:T(8,128)(2,1)S(1)}, bf16[128,2048]{1,0:T(8,128)(2,1)S(1)}, u32[]{:S(2)}, u32[]{:S(2)}) collective-permute-start(bf16[128,2048]{1,0:T(8,128)(2,1)S(1)} %add_convert_fusion.1), channel_id=1, source_target_pairs={{0,4},{1,5},{4,8},{5,9},{8,12},{9,13},{12,14},{13,15},{14,10},{15,... | collective-permute-start | bytes 1572872 | tf_op jit(solution)/shard_map/ppermute | solution.py:294
  (2 other events, 1.7 us)
